TPU v7x, 32 devices: a whole 2x2x4 slice. The times are simulated.
32 devices in a mesh: section: 4 (over x, core), tp: 8 (over z, y).
Axes of the slice: x: 2, y: 2, z: 4, core: 2. Of those that a mesh axis runs over, the one named last changes fastest.
Arguments:
- patches: bfloat16 [2, 32, 4096], P(None, None, 'tp'), may hold values from -6 to 6
- table_ids: int32 [2, 32], replicated, may hold values from 0 to 32767
- lengths: int32 [2, 2], replicated, may hold values from 16 to 32
- embed_table: bfloat16 [32768, 4096], P('section', 'tp'), may hold values from -6 to 6
- norm_gain: bfloat16 [4, 4096], P('section'), may hold values from 0.099609375 to 1.8984375
- w_query: bfloat16 [4, 4096, 4096], P('section', None, 'tp'), may hold values from -0.09375 to 0.09375
- w_key: bfloat16 [4, 4096, 4096], P('section', None, 'tp'), may hold values from -0.09375 to 0.09375
- w_value: bfloat16 [4, 4096, 4096], P('section', None, 'tp'), may hold values from -0.09375 to 0.09375
- w_out: bfloat16 [4, 4096, 4096], P('section', None, 'tp'), may hold values from -0.09375 to 0.09375
Outputs:
- layer_rows: bfloat16 [4, 2, 32, 4096], P('section', None, None, 'tp')
Inputs may be any that keep to these rules, and one draw needn't show every extreme that they name: `lengths`: column 0 counts a micro-batch's valid patches, column 1 its valid table tokens.
All inputs are finite; a program needn't handle non-finite values.
Results may differ from a plain program's by a relative error of at most 0.01.
Values may be sent and summed in bfloat16 or wider, within the bound.
No kernel may reach another device: no remote copies, remote signals or barrier semaphores. Data moves between devices by JAX's collectives and lax.ppermute only.
A program may use at most 64 MiB of HBM per device.

v0:
```python
import math

import jax
import jax.numpy as jnp
from jax import lax
from jax.sharding import PartitionSpec as P

HEADS = 32


epsilon = 1e-06


def shifted(block, axis, distance):
    devices = range(lax.axis_size(axis))
    route = [(i - distance, i) for i in devices if i - distance in devices]
    return lax.ppermute(block, axis, route)


def local(patches, table_ids, lengths, embed_table, norm_gain, w_query, w_key, w_value, w_out):
    section_count = lax.axis_size("section")
    section_index = lax.axis_index("section")
    is_encoder = section_index < section_count // 2
    micro_count, row_count, width_local = patches.shape
    width_full = w_query.shape[1]
    head_dim = width_full // HEADS
    heads_local = width_local // head_dim
    score_scale = 1.0 / math.sqrt(head_dim)
    query_weight = w_query[0]
    key_weight = w_key[0]
    value_weight = w_value[0]
    out_weight = w_out[0]
    gain_row = norm_gain[0].astype(jnp.float32)
    vocab_local = embed_table.shape[0]
    local_ids = table_ids.reshape(-1) - section_index * vocab_local
    vocab_cols = lax.broadcasted_iota(jnp.int32, (local_ids.shape[0], vocab_local), 1)
    one_hot = (local_ids[:, None] == vocab_cols).astype(jnp.bfloat16)
    looked_up = jnp.dot(one_hot, embed_table, preferred_element_type=jnp.float32)
    embedded = lax.psum(looked_up.astype(jnp.bfloat16), "section")
    embedded = embedded.reshape(micro_count, row_count, width_local)
    first_inputs = jnp.concatenate([patches, embedded], axis=1)
    query_pos = lax.broadcasted_iota(jnp.int32, (row_count, 2 * row_count), 0)
    key_pos = lax.broadcasted_iota(jnp.int32, (row_count, 2 * row_count), 1)

    def head_outputs(full_rows, batch_index):
        values_f = full_rows.astype(jnp.float32)
        inverse = lax.rsqrt(jnp.mean(values_f * values_f, axis=-1, keepdims=True) + epsilon)
        normed = (values_f * inverse * gain_row).astype(jnp.bfloat16)
        own_rows = jnp.where(is_encoder, normed[:row_count], normed[row_count:])
        query = (
            jnp.dot(own_rows, query_weight, preferred_element_type=jnp.float32) * score_scale
        ).astype(jnp.bfloat16)
        key_rows = jnp.dot(normed, key_weight, preferred_element_type=jnp.float32).astype(
            jnp.bfloat16
        )
        value_rows = jnp.dot(normed, value_weight, preferred_element_type=jnp.float32).astype(
            jnp.bfloat16
        )
        query_heads = query.reshape(row_count, heads_local, head_dim)
        key_heads = key_rows.reshape(2 * row_count, heads_local, head_dim)
        value_heads = value_rows.reshape(2 * row_count, heads_local, head_dim)
        scores = jnp.einsum(
            "qhd,khd->hqk", query_heads, key_heads, preferred_element_type=jnp.float32
        )
        patch_count = lengths[batch_index, 0]
        table_count = lengths[batch_index, 1]
        patch_mask = (key_pos < row_count) & (key_pos < patch_count)
        table_mask = (
            (key_pos >= row_count)
            & (key_pos - row_count <= query_pos)
            & (key_pos - row_count < table_count)
        )
        key_mask = jnp.where(is_encoder, patch_mask, patch_mask | table_mask)
        exp_scores = jnp.where(key_mask[None], jnp.exp(scores), 0.0)
        weights = (exp_scores / jnp.sum(exp_scores, axis=-1, keepdims=True)).astype(jnp.bfloat16)
        head_mix = jnp.einsum(
            "hqk,khd->qhd", weights, value_heads, preferred_element_type=jnp.float32
        )
        return head_mix.astype(jnp.bfloat16).reshape(row_count, width_local)

    def add_block(piece):
        return jnp.dot(piece, out_weight, preferred_element_type=jnp.float32)

    def project_heads(head_mix):
        return add_block(lax.all_gather(head_mix, "tp", axis=1, tiled=True))

    def pass_on(stream):
        return shifted(stream, "section", 1)

    def place_rows(stream, updated):
        with_patches = jnp.concatenate([updated, stream[row_count:]], axis=0)
        with_table = jnp.concatenate([stream[:row_count], updated], axis=0)
        return jnp.where(is_encoder, with_patches, with_table)

    stash = jnp.zeros((micro_count, row_count, width_local), jnp.bfloat16)
    step_count = micro_count + section_count - 1

    def advance(step_index, carry):
        incoming, stash_rows = carry
        batch_index = step_index - section_index
        active = (batch_index >= 0) & (batch_index < micro_count)
        batch_index = jnp.clip(batch_index, 0, micro_count - 1)
        first_input = lax.dynamic_index_in_dim(first_inputs, batch_index, 0, keepdims=False)
        stream = jnp.where(section_index == 0, first_input, incoming)
        full_rows = lax.all_gather(stream, "tp", axis=1, tiled=True)
        change = project_heads(head_outputs(full_rows, batch_index))
        residual = jnp.where(is_encoder, stream[:row_count], stream[row_count:])
        updated = (residual.astype(jnp.float32) + change).astype(jnp.bfloat16)
        stored = lax.dynamic_update_index_in_dim(stash_rows, updated, batch_index, 0)
        stash_rows = jnp.where(active, stored, stash_rows)
        return (pass_on(place_rows(stream, updated)), stash_rows)

    start_stream = jnp.zeros((2 * row_count, width_local), jnp.bfloat16)
    final_carry = lax.fori_loop(0, step_count, advance, (start_stream, stash))
    return final_carry[1][None]


def solution(mesh):
    return jax.shard_map(
        local,
        mesh=mesh,
        in_specs=(
            P(None, None, "tp"),
            P(),
            P(),
            P("section", "tp"),
            P("section", None),
            P("section", None, "tp"),
            P("section", None, "tp"),
            P("section", None, "tp"),
            P("section", None, "tp"),
        ),
        out_specs=P("section", None, None, "tp"),
        check_vma=False,
    )
```

profile of v0, /device:TPU:3, one launch (start us, length us, event | category | flops | bytes accessed | tf_op | source)
XLA Modules:
  0.0 443.9 jit_solution(11587463912320818533)
XLA Ops:
  7.3 5.7 %fusion.32 = bf16[64,512]{1,0:T(8,128)(2,1)} fusion(bf16[8192,512]{1,0:T(8,128)(2,1)} %param.14, s32[64]{0:T(128)S(1)} %sub.33), kind=kOutput, calls=%fused_computation.52 | convolution fusion | flops 537427968 | bytes 8454400 | tf_op jit(solution)/shard_map/dot_general | solution.py:38
  13.0 31.1 %all-reduce.2.cloned.1.call-done = bf16[2,32,512]{2,1,0:T(8,128)(2,1)} async-done(((bf16[2,32,512]{2,1,0:T(8,128)(2,1)}), bf16[2,32,512]{2,1,0:T(8,128)(2,1)}) %all-reduce.2.cloned.1.call-update) | async-done | bytes 65552 | tf_op jit(solution)/shard_map/psum | solution.py:39
  44.2 0.8 pad_maximum_fusion
  45.1 391.4 %while.19 = (s32[]{:T(128)}, bf16[64,512]{1,0:T(8,128)(2,1)S(1)}, bf16[2,32,512]{2,1,0:T(8,128)(2,1)S(1)}, pred[]{:T(512)}, pred[]{:T(512)}, /*index=5*/s32[]{:T...) while((s32[]{:T(128)}, bf16[64,512]{1,0:T(8,128)(2,1)S(1)}, ...), condition=%wide.region_4.5_spmd.clone.clone, body=%wide.region_1.4_spmd.clone.clone.sunk | while | flops 812038400 | bytes 56055120 | solution.py:114
  45.1 25.0 %all_gather.26 = bf16[64,4096]{1,0:T(8,128)(2,1)S(1)} all-gather(bf16[64,512]{1,0:T(8,128)(2,1)S(1)} %bitcast_select_fusion.3), channel_id=1, replica_groups=mesh['section'=4,'tp'=8] {'tp'}, dimensions={1}, use_global_device_ids=true | all-gather | bytes 589824 | tf_op jit(solution)/shard_map/while/body/eval_jaxpr/all_gather | solution.py:105
  71.2 3.2 fusion.79
  74.4 0.8 fusion.78
  75.2 0.8 fusion.80
  76.0 1.2 or_select_fusion.2
  77.7 24.5 %all_gather.27 = bf16[32,4096]{1,0:T(8,128)(2,1)S(1)} all-gather(bf16[32,512]{1,0:T(8,128)(2,1)S(1)} %bitcast.89), channel_id=1, replica_groups=mesh['section'=4,'tp'=8] {'tp'}, dimensions={1}, use_global_device_ids=true | all-gather | bytes 294912 | tf_op jit(solution)/shard_map/while/body/eval_jaxpr/all_gather | solution.py:85
  102.2 3.0 fusion.83
  105.3 1.3 collective-permute-start
  106.6 15.3 %collective-permute-done = bf16[64,512]{1,0:T(8,128)(2,1)S(1)} collective-permute-done((bf16[64,512]{1,0:T(8,128)(2,1)S(1)}, bf16[64,512]{1,0:T(8,128)(2,1)S(1)}, u32[]{:S(2)}, u32[]{:S(2)}) %collective-permute-start) | collective-permute-done | bytes 65568 | tf_op jit(solution)/shard_map/while/body/eval_jaxpr/ppermute | solution.py:17
  121.9 25.8 %all_gather.26 = bf16[64,4096]{1,0:T(8,128)(2,1)S(1)} all-gather(bf16[64,512]{1,0:T(8,128)(2,1)S(1)} %bitcast_select_fusion.3), channel_id=1, replica_groups=mesh['section'=4,'tp'=8] {'tp'}, dimensions={1}, use_global_device_ids=true | all-gather | bytes 589824 | tf_op jit(solution)/shard_map/while/body/eval_jaxpr/all_gather | solution.py:105
  148.7 3.2 fusion.79
  151.9 0.8 fusion.78
  152.8 0.8 fusion.80
  153.6 1.2 or_select_fusion.2
  155.2 24.4 %all_gather.27 = bf16[32,4096]{1,0:T(8,128)(2,1)S(1)} all-gather(bf16[32,512]{1,0:T(8,128)(2,1)S(1)} %bitcast.89), channel_id=1, replica_groups=mesh['section'=4,'tp'=8] {'tp'}, dimensions={1}, use_global_device_ids=true | all-gather | bytes 294912 | tf_op jit(solution)/shard_map/while/body/eval_jaxpr/all_gather | solution.py:85
  179.6 3.0 fusion.83
  182.6 1.3 collective-permute-start
  184.0 16.6 %collective-permute-done = bf16[64,512]{1,0:T(8,128)(2,1)S(1)} collective-permute-done((bf16[64,512]{1,0:T(8,128)(2,1)S(1)}, bf16[64,512]{1,0:T(8,128)(2,1)S(1)}, u32[]{:S(2)}, u32[]{:S(2)}) %collective-permute-start) | collective-permute-done | bytes 65568 | tf_op jit(solution)/shard_map/while/body/eval_jaxpr/ppermute | solution.py:17
  200.6 25.8 %all_gather.26 = bf16[64,4096]{1,0:T(8,128)(2,1)S(1)} all-gather(bf16[64,512]{1,0:T(8,128)(2,1)S(1)} %bitcast_select_fusion.3), channel_id=1, replica_groups=mesh['section'=4,'tp'=8] {'tp'}, dimensions={1}, use_global_device_ids=true | all-gather | bytes 589824 | tf_op jit(solution)/shard_map/while/body/eval_jaxpr/all_gather | solution.py:105
  227.4 3.2 fusion.79
  230.6 0.8 fusion.78
  231.4 0.8 fusion.80
  232.3 1.2 or_select_fusion.2
  233.9 24.4 %all_gather.27 = bf16[32,4096]{1,0:T(8,128)(2,1)S(1)} all-gather(bf16[32,512]{1,0:T(8,128)(2,1)S(1)} %bitcast.89), channel_id=1, replica_groups=mesh['section'=4,'tp'=8] {'tp'}, dimensions={1}, use_global_device_ids=true | all-gather | bytes 294912 | tf_op jit(solution)/shard_map/while/body/eval_jaxpr/all_gather | solution.py:85
  258.3 3.0 fusion.83
  261.3 1.3 collective-permute-start
  262.6 16.5 %collective-permute-done = bf16[64,512]{1,0:T(8,128)(2,1)S(1)} collective-permute-done((bf16[64,512]{1,0:T(8,128)(2,1)S(1)}, bf16[64,512]{1,0:T(8,128)(2,1)S(1)}, u32[]{:S(2)}, u32[]{:S(2)}) %collective-permute-start) | collective-permute-done | bytes 65568 | tf_op jit(solution)/shard_map/while/body/eval_jaxpr/ppermute | solution.py:17
  279.1 25.8 %all_gather.26 = bf16[64,4096]{1,0:T(8,128)(2,1)S(1)} all-gather(bf16[64,512]{1,0:T(8,128)(2,1)S(1)} %bitcast_select_fusion.3), channel_id=1, replica_groups=mesh['section'=4,'tp'=8] {'tp'}, dimensions={1}, use_global_device_ids=true | all-gather | bytes 589824 | tf_op jit(solution)/shard_map/while/body/eval_jaxpr/all_gather | solution.py:105
  305.9 3.2 fusion.79
  309.1 0.8 fusion.78
  310.8 1.2 or_select_fusion.2
  312.4 24.4 %all_gather.27 = bf16[32,4096]{1,0:T(8,128)(2,1)S(1)} all-gather(bf16[32,512]{1,0:T(8,128)(2,1)S(1)} %bitcast.89), channel_id=1, replica_groups=mesh['section'=4,'tp'=8] {'tp'}, dimensions={1}, use_global_device_ids=true | all-gather | bytes 294912 | tf_op jit(solution)/shard_map/while/body/eval_jaxpr/all_gather | solution.py:85
  336.8 3.0 fusion.83
  339.8 1.3 collective-permute-start
  341.1 16.6 %collective-permute-done = bf16[64,512]{1,0:T(8,128)(2,1)S(1)} collective-permute-done((bf16[64,512]{1,0:T(8,128)(2,1)S(1)}, bf16[64,512]{1,0:T(8,128)(2,1)S(1)}, u32[]{:S(2)}, u32[]{:S(2)}) %collective-permute-start) | collective-permute-done | bytes 65568 | tf_op jit(solution)/shard_map/while/body/eval_jaxpr/ppermute | solution.py:17
  357.8 25.8 %all_gather.26 = bf16[64,4096]{1,0:T(8,128)(2,1)S(1)} all-gather(bf16[64,512]{1,0:T(8,128)(2,1)S(1)} %bitcast_select_fusion.3), channel_id=1, replica_groups=mesh['section'=4,'tp'=8] {'tp'}, dimensions={1}, use_global_device_ids=true | all-gather | bytes 589824 | tf_op jit(solution)/shard_map/while/body/eval_jaxpr/all_gather | solution.py:105
  384.5 3.2 fusion.79
  387.7 0.8 fusion.78
  388.6 0.8 fusion.80
  389.4 1.2 or_select_fusion.2
  391.0 24.4 %all_gather.27 = bf16[32,4096]{1,0:T(8,128)(2,1)S(1)} all-gather(bf16[32,512]{1,0:T(8,128)(2,1)S(1)} %bitcast.89), channel_id=1, replica_groups=mesh['section'=4,'tp'=8] {'tp'}, dimensions={1}, use_global_device_ids=true | all-gather | bytes 294912 | tf_op jit(solution)/shard_map/while/body/eval_jaxpr/all_gather | solution.py:85
  415.4 3.0 fusion.83
  418.5 1.3 collective-permute-start
  419.8 16.7 %collective-permute-done = bf16[64,512]{1,0:T(8,128)(2,1)S(1)} collective-permute-done((bf16[64,512]{1,0:T(8,128)(2,1)S(1)}, bf16[64,512]{1,0:T(8,128)(2,1)S(1)}, u32[]{:S(2)}, u32[]{:S(2)}) %collective-permute-start) | collective-permute-done | bytes 65568 | tf_op jit(solution)/shard_map/while/body/eval_jaxpr/ppermute | solution.py:17
  (86 shorter events, 9.3 us)
Async XLA Ops:
  6.5 37.6 %all-reduce.2.cloned.1.call-start = ((), (), s32[]{:S(2)}) async-start(), calls=%async_computation | async-start | bytes 131072 | tf_op jit(solution)/shard_map/psum | solution.py:39
  7.3 5.7 %copy-start.5 = (bf16[1,4096]{1,0:T(2,128)(2,1)S(1)}, bf16[1,4096]{1,0:T(2,128)(2,1)}, u32[]{:S(2)}) copy-start(bf16[1,4096]{1,0:T(2,128)(2,1)} %param.15) | copy-start | bytes 24580
  7.3 36.9 %copy-start.3 = (bf16[2,32,512]{2,1,0:T(8,128)(2,1)S(1)}, bf16[2,32,512]{2,1,0:T(8,128)(2,1)}, u32[]{:S(2)}) copy-start(bf16[2,32,512]{2,1,0:T(8,128)(2,1)} %param.11) | copy-start | bytes 196612
  7.3 37.8 %copy-start.4 = (s32[2,2]{1,0:T(2,128)S(1)}, s32[2,2]{1,0:T(2,128)}, u32[]{:S(2)}) copy-start(s32[2,2]{1,0:T(2,128)} %param.13) | copy-start | bytes 52
  45.1 29.3 %copy-start = (bf16[4096,512]{1,0:T(8,128)(2,1)S(1)}, bf16[4096,512]{1,0:T(8,128)(2,1)}, u32[]{:S(2)}) copy-start(bf16[4096,512]{1,0:T(8,128)(2,1)} %get-tuple-element.579) | copy-start | bytes 12582916 | tf_op jit(solution)/shard_map/while
  71.2 4.0 copy-start.1
  105.3 16.7 %collective-permute-start = (bf16[64,512]{1,0:T(8,128)(2,1)S(1)}, bf16[64,512]{1,0:T(8,128)(2,1)S(1)}, u32[]{:S(2)}, u32[]{:S(2)}) collective-permute-start(bf16[64,512]{1,0:T(8,128)(2,1)S(1)} %maximum_select_fusion.2), channel_id=1, source_target_pairs={{0,8},{8,16},{16,24},{1,9},{9,17},{17,25},{2,10},{10,18},{18,26},{... | collective-permute-start | bytes 196616 | tf_op jit(solution)/shard_map/while/body/eval_jaxpr/ppermute | solution.py:17
  121.9 30.0 %copy-start = (bf16[4096,512]{1,0:T(8,128)(2,1)S(1)}, bf16[4096,512]{1,0:T(8,128)(2,1)}, u32[]{:S(2)}) copy-start(bf16[4096,512]{1,0:T(8,128)(2,1)} %get-tuple-element.579) | copy-start | bytes 12582916 | tf_op jit(solution)/shard_map/while
  148.7 4.0 copy-start.1
  182.6 17.9 %collective-permute-start = (bf16[64,512]{1,0:T(8,128)(2,1)S(1)}, bf16[64,512]{1,0:T(8,128)(2,1)S(1)}, u32[]{:S(2)}, u32[]{:S(2)}) collective-permute-start(bf16[64,512]{1,0:T(8,128)(2,1)S(1)} %maximum_select_fusion.2), channel_id=1, source_target_pairs={{0,8},{8,16},{16,24},{1,9},{9,17},{17,25},{2,10},{10,18},{18,26},{... | collective-permute-start | bytes 196616 | tf_op jit(solution)/shard_map/while/body/eval_jaxpr/ppermute | solution.py:17
  200.5 30.0 %copy-start = (bf16[4096,512]{1,0:T(8,128)(2,1)S(1)}, bf16[4096,512]{1,0:T(8,128)(2,1)}, u32[]{:S(2)}) copy-start(bf16[4096,512]{1,0:T(8,128)(2,1)} %get-tuple-element.579) | copy-start | bytes 12582916 | tf_op jit(solution)/shard_map/while
  227.4 4.0 copy-start.1
  261.3 17.8 %collective-permute-start = (bf16[64,512]{1,0:T(8,128)(2,1)S(1)}, bf16[64,512]{1,0:T(8,128)(2,1)S(1)}, u32[]{:S(2)}, u32[]{:S(2)}) collective-permute-start(bf16[64,512]{1,0:T(8,128)(2,1)S(1)} %maximum_select_fusion.2), channel_id=1, source_target_pairs={{0,8},{8,16},{16,24},{1,9},{9,17},{17,25},{2,10},{10,18},{18,26},{... | collective-permute-start | bytes 196616 | tf_op jit(solution)/shard_map/while/body/eval_jaxpr/ppermute | solution.py:17
  279.1 30.0 %copy-start = (bf16[4096,512]{1,0:T(8,128)(2,1)S(1)}, bf16[4096,512]{1,0:T(8,128)(2,1)}, u32[]{:S(2)}) copy-start(bf16[4096,512]{1,0:T(8,128)(2,1)} %get-tuple-element.579) | copy-start | bytes 12582916 | tf_op jit(solution)/shard_map/while
  305.9 4.0 copy-start.1
  339.8 17.9 %collective-permute-start = (bf16[64,512]{1,0:T(8,128)(2,1)S(1)}, bf16[64,512]{1,0:T(8,128)(2,1)S(1)}, u32[]{:S(2)}, u32[]{:S(2)}) collective-permute-start(bf16[64,512]{1,0:T(8,128)(2,1)S(1)} %maximum_select_fusion.2), channel_id=1, source_target_pairs={{0,8},{8,16},{16,24},{1,9},{9,17},{17,25},{2,10},{10,18},{18,26},{... | collective-permute-start | bytes 196616 | tf_op jit(solution)/shard_map/while/body/eval_jaxpr/ppermute | solution.py:17
  357.7 30.0 %copy-start = (bf16[4096,512]{1,0:T(8,128)(2,1)S(1)}, bf16[4096,512]{1,0:T(8,128)(2,1)}, u32[]{:S(2)}) copy-start(bf16[4096,512]{1,0:T(8,128)(2,1)} %get-tuple-element.579) | copy-start | bytes 12582916 | tf_op jit(solution)/shard_map/while
  384.5 4.0 copy-start.1
  418.5 18.0 %collective-permute-start = (bf16[64,512]{1,0:T(8,128)(2,1)S(1)}, bf16[64,512]{1,0:T(8,128)(2,1)S(1)}, u32[]{:S(2)}, u32[]{:S(2)}) collective-permute-start(bf16[64,512]{1,0:T(8,128)(2,1)S(1)} %maximum_select_fusion.2), channel_id=1, source_target_pairs={{0,8},{8,16},{16,24},{1,9},{9,17},{17,25},{2,10},{10,18},{18,26},{... | collective-permute-start | bytes 196616 | tf_op jit(solution)/shard_map/while/body/eval_jaxpr/ppermute | solution.py:17
  436.4 0.6 copy-start.2
Sparse Core Ops, SparseCore 0:
  13.1 31.0 all-reduce.1
where the time goes:
time: 447 us; the launch traced here: 444 us
  blocking collectives  250 us (56%)
  waiting for transfers between devices  113 us (25%)
  matrix products  46.6 us (10%)
  between operations  13.4 us (3%)
  other arithmetic  9.88 us (2%)
  starting transfers between devices  6.46 us (1%)
    all_gather x5, blocking collectives, advance(): full_rows = lax.all_gather(stream, 'tp', axis=1, tiled=True)  128 us
    all_gather x5, blocking collectives, project_heads(): return add_block(lax.all_gather(head_mix, 'tp', axis=1, tiled=True))  122 us
    ppermute x5, waiting for transfers between devices, shifted(): return lax.ppermute(block, axis, route)  81.7 us
    psum x1, waiting for transfers between devices, local(): embedded = lax.psum(looked_up.astype(jnp.bfloat16), 'section')  31.1 us
    dot_general x5, matrix products, head_outputs(): jnp.dot(normed, key_weight, preferred_element_type=jnp.float32)  15.9 us
    dot_general x5, matrix products, add_block(): return jnp.dot(piece, out_weight, preferred_element_type=jnp.float32)  15 us
  transfers between devices with their start and end apart: 6, of which 6 were waited for; matrix products, arithmetic and copies ran while one was open for 0% of the time, Pallas kernels for 0%

commit v1 on v0

v1 whole, which is shorter than its diff:
```python
import math

import jax
import jax.numpy as jnp
from jax import lax
from jax.sharding import PartitionSpec as P

HEADS = 32


epsilon = 1e-06


def xor_groups(count):
    bits = [1 << i for i in reversed(range(count.bit_length() - 1))]
    first = len(bits) % 2
    groups = [bits[:first]] if first else []
    return groups + [bits[i : i + 2] for i in range(first, len(bits), 2)]


def gather_rows(block, axis):
    count = lax.axis_size(axis)
    me = lax.axis_index(axis)
    if count & (count - 1):
        return lax.all_gather(block, axis, axis=0, tiled=False)
    held = block[None]
    for bits in xor_groups(count):
        masks = [0]
        for bit in bits:
            masks = masks + [mask | bit for mask in masks]
        pieces = {0: held}
        for mask in sorted(masks[1:], reverse=True):
            route = [(i, i ^ mask) for i in range(count)]
            pieces[mask] = lax.ppermute(held, axis, route)
        for bit in bits:
            swap = (me & bit) != 0
            pieces = {
                mask: jnp.where(swap, pieces[mask ^ bit], pieces[mask]) for mask in pieces
            }
        held = jnp.stack([pieces[mask] for mask in sorted(masks)], axis=0)
    groups = xor_groups(count)
    shape = []
    for bits in reversed(groups):
        shape.append(1 << len(bits))
    held = held.reshape(tuple(shape) + block.shape)
    order = tuple(reversed(range(len(shape)))) + (len(shape), len(shape) + 1)
    return held.transpose(order).reshape((count,) + block.shape)


def side_by_side(stacked):
    count, rows, width = stacked.shape
    return stacked.transpose(1, 0, 2).reshape(rows, count * width)


def exchange(block, axis, first, second):
    index = lax.axis_index(axis)
    route = [(first, second), (second, first)]
    return lax.cond(
        (index == first) | (index == second),
        lambda rows: lax.ppermute(rows, axis, route),
        lambda rows: rows,
        block,
    )


def local(patches, table_ids, lengths, embed_table, norm_gain, w_query, w_key, w_value, w_out):
    section_count = lax.axis_size("section")
    section_index = lax.axis_index("section")
    half = section_count // 2
    micro_count, row_count, width_local = patches.shape
    width_full = w_query.shape[1]
    head_dim = width_full // HEADS
    heads_local = width_local // head_dim
    score_scale = 1.0 / math.sqrt(head_dim)
    query_weight = w_query[0]
    key_weight = w_key[0]
    value_weight = w_value[0]
    out_weight = w_out[0]
    gain_row = norm_gain[0].astype(jnp.float32)
    total_rows = micro_count * row_count
    vocab_local = embed_table.shape[0]

    def only(indices, body, operands, shape):
        taken = section_index == indices[0]
        for index in indices[1:]:
            taken = taken | (section_index == index)
        return lax.cond(taken, body, lambda *_: tuple(jnp.zeros(s, d) for s, d in shape), *operands)

    def look_up():
        local_ids = table_ids.reshape(-1) - section_index * vocab_local
        vocab_cols = lax.broadcasted_iota(jnp.int32, (total_rows, vocab_local), 1)
        one_hot = (local_ids[:, None] == vocab_cols).astype(jnp.bfloat16)
        return jnp.dot(one_hot, embed_table, preferred_element_type=jnp.float32).astype(
            jnp.bfloat16
        )

    def normalise(full):
        values_f = full.astype(jnp.float32)
        inverse = lax.rsqrt(jnp.mean(values_f * values_f, axis=-1, keepdims=True) + epsilon)
        return (values_f * inverse * gain_row).astype(jnp.bfloat16)

    def project(normed, weight):
        return jnp.dot(normed, weight, preferred_element_type=jnp.float32)

    def heads_of(rows):
        return rows.reshape(micro_count, row_count, heads_local, head_dim)

    def attend(query, keys, values, mask):
        scores = jnp.einsum("mqhd,mkhd->mhqk", query, keys, preferred_element_type=jnp.float32)
        exp_scores = jnp.where(mask[:, None], jnp.exp(scores), 0.0)
        weights = (exp_scores / jnp.sum(exp_scores, axis=-1, keepdims=True)).astype(jnp.bfloat16)
        mix = jnp.einsum("mhqk,mkhd->mqhd", weights, values, preferred_element_type=jnp.float32)
        return mix.astype(jnp.bfloat16).reshape(total_rows, width_local)

    def gathered(block):
        return side_by_side(gather_rows(block, "tp"))

    def finish(stream, mix):
        change = project(gathered(mix), out_weight)
        return (stream.astype(jnp.float32) + change).astype(jnp.bfloat16)

    def patch_mask(shape):
        key_pos = lax.broadcasted_iota(jnp.int32, shape, 2)
        return key_pos < lengths[:, 0][:, None, None]

    def encode(stream):
        normed = normalise(gathered(stream))
        query = heads_of((project(normed, query_weight) * score_scale).astype(jnp.bfloat16))
        keys = heads_of(project(normed, key_weight).astype(jnp.bfloat16))
        values = heads_of(project(normed, value_weight).astype(jnp.bfloat16))
        mask = patch_mask((micro_count, row_count, row_count))
        return (finish(stream, attend(query, keys, values, mask)),)

    def memory_rows(memory_full):
        normed = normalise(memory_full)
        keys = project(normed, key_weight).astype(jnp.bfloat16)
        values = project(normed, value_weight).astype(jnp.bfloat16)
        return keys, values

    def table_rows(stream):
        normed = normalise(gathered(stream))
        query = (project(normed, query_weight) * score_scale).astype(jnp.bfloat16)
        keys = project(normed, key_weight).astype(jnp.bfloat16)
        values = project(normed, value_weight).astype(jnp.bfloat16)
        return query, keys, values

    def decode(stream, memory_keys, memory_values, query, keys, values):
        shape = (micro_count, row_count, row_count)
        query_pos = lax.broadcasted_iota(jnp.int32, shape, 1)
        key_pos = lax.broadcasted_iota(jnp.int32, shape, 2)
        own = (key_pos <= query_pos) & (key_pos < lengths[:, 1][:, None, None])
        mask = jnp.concatenate([patch_mask(shape), own], axis=2)
        all_keys = jnp.concatenate([heads_of(memory_keys), heads_of(keys)], axis=1)
        all_values = jnp.concatenate([heads_of(memory_values), heads_of(values)], axis=1)
        mix = attend(heads_of(query), all_keys, all_values, mask)
        return (finish(stream, mix),)

    bf16 = jnp.bfloat16
    part = ((total_rows, width_local), bf16)
    whole = ((total_rows, width_full), bf16)

    def after(value, *earlier):
        return lax.optimization_barrier((value,) + earlier)[0]

    stream = patches.reshape(total_rows, width_local)
    (updated,) = only([0], encode, (stream,), (part,))
    result = updated
    rows_found = lax.cond(section_index != 0, look_up, lambda: jnp.zeros(*part))
    for index in range(1, section_count):
        if index != half:
            sent = exchange(rows_found, "section", index, half)
            rows_found = jnp.where(section_index == half, rows_found + sent, rows_found)
    stream = exchange(updated, "section", 0, 1)
    rows_found, stream = lax.optimization_barrier((rows_found, stream))
    own_found = lax.cond(section_index == 0, look_up, lambda: rows_found)
    sent = exchange(own_found, "section", 0, half)
    embedded = own_found + sent
    table = only([half], table_rows, (embedded,), (part, part, part))
    for index in range(1, half):
        (updated,) = only([index], encode, (stream,), (part,))
        result = jnp.where(section_index == index, updated, result)
        stream = exchange(updated, "section", index, index + 1)

    (memory,) = only([half], lambda block: (gathered(block),), (stream,), (whole,))
    stream = embedded
    for index in range(half, section_count):
        if index > half:
            memory_next = exchange(memory, "section", index - 1, index)
            memory = jnp.where(section_index == index, memory_next, memory)
        pair = only([index], memory_rows, (memory,), (part, part))
        if index > half:
            stream = exchange(after(stream, *pair), "section", index - 1, index)
            table = only([index], table_rows, (stream,), (part, part, part))
        (updated,) = only([index], decode, (stream, *pair, *table), (part,))
        result = jnp.where(section_index == index, updated, result)
        stream = updated
    return result.reshape(1, micro_count, row_count, width_local)


def solution(mesh):
    return jax.shard_map(
        local,
        mesh=mesh,
        in_specs=(
            P(None, None, "tp"),
            P(),
            P(),
            P("section", "tp"),
            P("section", None),
            P("section", None, "tp"),
            P("section", None, "tp"),
            P("section", None, "tp"),
            P("section", None, "tp"),
        ),
        out_specs=P("section", None, None, "tp"),
        check_vma=False,
    )
```

time: 447 us -> 190 us (0.43)
  blocking collectives: 250 us -> 0 us
  starting transfers between devices: 6.46 us -> 145 us
  waiting for transfers between devices: 113 us -> 16 us
  matrix products: 46.6 us -> 14.8 us
  between operations: 13.4 us -> 0.14 us
    all_gather x10 -> x0, blocking collectives: 250 us -> none  [the longest x5 128 us: advance(): full_rows = lax.all_gather(stream, 'tp', axis=1, tiled=True)]
    ppermute x5 -> x11, starting transfers between devices: 6.46 us -> 145 us  [the longest x3 136 us: exchange(): lax.ppermute(rows, axis, route)]
    ppermute x5 -> x11, waiting for transfers between devices: 81.7 us -> 16 us  [the longest x8 12 us: gather_rows(): pieces[mask] = lax.ppermute(held, axis, route)]
    dot_general x31 -> x9, matrix products: 46.6 us -> 14.8 us  [the longest x6 9.39 us: project(): return jnp.dot(normed, weight, preferred_element_type=jnp.float32)]
    psum x1 -> x0, waiting for transfers between devices: 31.1 us -> none  [local(): embedded = lax.psum(looked_up.astype(jnp.bfloat16), 'section')]
  transfers between devices with their start and end apart: 6 -> 11, of which waited for: 6 -> 11; matrix products, arithmetic and copies ran while one was open for 0% -> 0% of each run, Pallas kernels for 0% -> 0%
where the time goes in v1:
time: 190 us; the launch traced here: 189 us
  starting transfers between devices  145 us (76%)
  waiting for transfers between devices  16 us (8%)
  matrix products  14.8 us (8%)
  other arithmetic  7.81 us (4%)
  local copies, waits for them, and re-layouts  4.76 us (3%)
    ppermute x3, starting transfers between devices, exchange(): lax.ppermute(rows, axis, route)  136 us
    ppermute x8, waiting for transfers between devices, gather_rows(): pieces[mask] = lax.ppermute(held, axis, route)  12 us
    dot_general x6, matrix products, project(): return jnp.dot(normed, weight, preferred_element_type=jnp.float32)  9.39 us
    ppermute x8, starting transfers between devices, gather_rows(): pieces[mask] = lax.ppermute(held, axis, route)  9.04 us
    dot_general x1, matrix products, look_up(): jnp.dot(one_hot, embed_table, preferred_element_type=jnp.float32)  4.99 us
    cond x14, local copies, waits for them, and re-layouts  4.07 us
    ppermute x3, waiting for transfers between devices, exchange(): lax.ppermute(rows, axis, route)  4.01 us
  transfers between devices with their start and end apart: 11, of which 11 were waited for; matrix products, arithmetic and copies ran while one was open for 0% of the time, Pallas kernels for 0%

profile of v1, /device:TPU:3, one launch (start us, length us, event | category | flops | bytes accessed | tf_op | source)
XLA Modules:
  0.0 189.0 jit_solution(14010771331336674320)
XLA Ops:
  0.0 0.7 convert_element_type.282
  0.8 5.8 %conditional.18 = (bf16[64,512]{1,0:T(8,128)(2,1)S(1)}) conditional(s32[]{:T(128)} %convert_element_type.270, () %tuple.125, (s32[]{:T(128)}, s32[2,32]{1,0:T(2,128)}, bf16[8192,512]{1,0:T(8,128)(2,1)}) %tuple.126), branch_computations={%region_0.0_spmd, %region_1.2_spmd} | conditional | flops 537428032 | bytes 8455448 | solution.py:168
  0.8 0.7 broadcast_subtract_fusion
  1.6 5.0 %fusion.1 = bf16[64,512]{1,0:T(8,128)(2,1)S(1)} fusion(bf16[8192,512]{1,0:T(8,128)(2,1)} %get-tuple-element.181, s32[64]{0:T(128)S(1)} %sub.22), kind=kOutput, calls=%fused_computation.2 | convolution fusion | flops 537427968 | bytes 8454400 | tf_op jit(solution)/shard_map/cond/branch_1_fun/dot_general | solution.py:93
  6.6 0.6 conditional.22
  6.6 0.6 copy.303
  7.3 0.6 conditional.19
  7.9 0.8 add_select_fusion.1
  8.7 40.3 %conditional.20 = (bf16[64,512]{1,0:T(8,128)(2,1)}) conditional(s32[]{:T(128)} %convert_element_type.267, bf16[64,512]{1,0:T(8,128)(2,1)S(1)} %add_select_fusion.1, bf16[64,512]{1,0:T(8,128)(2,1)S(1)} %add_select_fusion.1), branch_computations={%region_4.5_spmd, %region_5.6_spmd} | conditional | bytes 262192 | solution.py:58
  8.8 39.2 %collective-permute-start.1 = (bf16[64,512]{1,0:T(8,128)(2,1)S(1)}, bf16[64,512]{1,0:T(8,128)(2,1)}, u32[]{:S(2)}, u32[]{:S(2)}) collective-permute-start(bf16[64,512]{1,0:T(8,128)(2,1)S(1)} %param.5), channel_id=1, source_target_pairs={{24,16},{16,24},{25,17},{17,25},{26,18},{18,26},{27,19},{19,27},{2... | collective-permute-start | bytes 196616 | tf_op jit(solution)/shard_map/cond/branch_1_fun/ppermute | solution.py:60
  48.0 1.0 collective-permute-done.1
  49.0 0.8 add_select_fusion
  49.9 0.6 conditional.26
  49.9 0.6 copy.311
  50.5 0.6 conditional.24
  50.5 0.6 copy.307
  51.2 0.9 add.71
  52.4 96.3 %conditional.31 = (bf16[64,4096]{1,0:T(8,128)(2,1)}) conditional(s32[]{:T(128)} %convert_element_type.267, bf16[64,4096]{1,0:T(8,128)(2,1)S(1)} %get-tuple-element.449, bf16[64,4096]{1,0:T(8,128)(2,1)S(1)} %get-tuple-element.449), branch_computations={%region_20.21_spmd, %region_21.22_spmd} | conditional | bytes 2097200 | solution.py:58
  52.4 94.6 %collective-permute-start.4 = (bf16[64,4096]{1,0:T(8,128)(2,1)S(1)}, bf16[64,4096]{1,0:T(8,128)(2,1)}, u32[]{:S(2)}, u32[]{:S(2)}) collective-permute-start(bf16[64,4096]{1,0:T(8,128)(2,1)S(1)} %param.17), channel_id=1, source_target_pairs={{16,24},{24,16},{17,25},{25,17},{18,26},{26,18},{19,27},{27,19},{2... | collective-permute-start | bytes 1572872 | tf_op jit(solution)/shard_map/cond/branch_1_fun/ppermute | solution.py:60
  147.1 1.6 collective-permute-done.4
  148.7 6.7 %conditional.32 = (bf16[64,512]{1,0:T(8,128)(2,1)S(1)}, bf16[64,512]{1,0:T(8,128)(2,1)S(1)}) conditional(s32[]{:T(128)} %convert_element_type.266, () %tuple.138, (pred[]{:T(512)}, bf16[64,4096]{1,0:T(8,128)(2,1)}, bf16[64,4096]{1,0:T(8,128)(2,1)S(1)}, f32[4096]{0:T(1024)S(1)}, bf16[4096,512]{1,0:T(8,128)(2,1)}, ...), branch_computations={%region_22.23_spmd, %region_23.25_spmd} | conditional | flops 540606528 | bytes 28476716 | solution.py:87
  148.7 1.5 fusion.27
  150.2 3.3 %convolution_convert_fusion.6 = bf16[64,512]{1,0:T(8,128)(2,1)S(1)} fusion(bf16[4096,512]{1,0:T(8,128)(2,1)} %get-tuple-element.202, f32[4096]{0:T(1024)S(1)} %get-tuple-element.200, f32[64]{0:T(128)S(1)} %add_rsqrt_fusion.2, bf16[64,4096]{1,0:T(8,128)(2,1)} %get-tuple-element.198, bf16[64,4096]{1,0:T(8,128)(2,1)S(1)} %get-tuple-element.199, ...), kind=kOutput, calls=%fused_computation.113 | convolution fusion | flops 269778944 | bytes 5325057 | tf_op jit(solution)/shard_map/cond/branch_1_fun/dot_general | solution.py:103
  153.5 2.0 %convolution_convert_fusion.7 = bf16[64,512]{1,0:T(8,128)(2,1)S(1)} fusion(bf16[4096,512]{1,0:T(8,128)(2,1)S(1)} %copy-done.8, f32[4096]{0:T(1024)S(1)} %get-tuple-element.200, f32[64]{0:T(128)S(1)} %add_rsqrt_fusion.2, bf16[64,4096]{1,0:T(8,128)(2,1)} %get-tuple-element.198, bf16[64,4096]{1,0:T(8,128)(2,1)S(1)} %get-tuple-element.199, pred[]{:T(512)} %get-tuple-element.197), kind=kOutput, calls=%fused_computation.114 | convolution fusion | flops 269778944 | bytes 5325057 | tf_op jit(solution)/shard_map/cond/branch_1_fun/dot_general | solution.py:103
  155.5 3.3 %conditional.33 = (bf16[64,512]{1,0:T(8,128)(2,1)}) conditional(s32[]{:T(128)} %convert_element_type.267, bf16[64,512]{1,0:T(8,128)(2,1)S(1)} %get-tuple-element.450, bf16[64,512]{1,0:T(8,128)(2,1)S(1)} %get-tuple-element.450), branch_computations={%region_38.39_spmd, %region_39.40_spmd} | conditional | bytes 262192 | solution.py:58
  155.5 1.9 %collective-permute-start.6 = (bf16[64,512]{1,0:T(8,128)(2,1)S(1)}, bf16[64,512]{1,0:T(8,128)(2,1)}, u32[]{:S(2)}, u32[]{:S(2)}) collective-permute-start(bf16[64,512]{1,0:T(8,128)(2,1)S(1)} %param.31), channel_id=1, source_target_pairs={{16,24},{24,16},{17,25},{25,17},{18,26},{26,18},{19,27},{27,19},{2... | collective-permute-start | bytes 196616 | tf_op jit(solution)/shard_map/cond/branch_1_fun/ppermute | solution.py:60
  157.4 1.4 collective-permute-done.6
  158.8 15.4 %conditional.34 = (bf16[64,512]{1,0:T(8,128)(2,1)S(1)}, bf16[64,512]{1,0:T(8,128)(2,1)S(1)}, bf16[64,512]{1,0:T(8,128)(2,1)S(1)}) conditional(s32[]{:T(128)} %convert_element_type.266, () %tuple.141, (bf16[64,512]{1,0:T(8,128)(2,1)}, f32[4096]{0:T(1024)S(1)}, bf16[4096,512]{1,0:T(8,128)(2,1)}, bf16[4096,512]{1,0:T(8,128)(2,1)}, ...), branch_computations={%region_40.41_spmd, %region_41.43_spmd} | conditional | flops 809566272 | bytes 73876840 | solution.py:87
  158.8 1.9 collective-permute-start.35
  160.6 2.6 %collective-permute-done.35 = bf16[1,64,512]{2,1,0:T(8,128)(2,1)S(1)} collective-permute-done((bf16[1,64,512]{2,1,0:T(8,128)(2,1)}, bf16[1,64,512]{2,1,0:T(8,128)(2,1)S(1)}, u32[]{:S(2)}, u32[]{:S(2)}) %collective-permute-start.35) | collective-permute-done | bytes 65568 | tf_op jit(solution)/shard_map/cond/branch_1_fun/ppermute | solution.py:34
  163.2 0.9 select_bitcast_fusion.45
  164.6 2.2 %collective-permute-start.36 = (bf16[2,1,64,512]{3,2,0,1:T(8,128)(2,1)S(1)}, bf16[2,1,64,512]{3,2,0,1:T(8,128)(2,1)S(1)}, u32[]{:S(2)}, u32[]{:S(2)}) collective-permute-start(bf16[2,1,64,512]{3,2,0,1:T(8,128)(2,1)S(1)} %pad_maximum_fusion.8), channel_id=1, source_target_pairs={{0,3},{1,2},{2,1},{3,0},{4,7},{5,6},{6,5},{7,4},{8,11},{9,10},{10,... | collective-permute-start | bytes 393224 | tf_op jit(solution)/shard_map/cond/branch_1_fun/ppermute | solution.py:34
  166.8 1.2 collective-permute-done.38
  168.0 1.4 collective-permute-done.36
  170.1 0.8 convolution_convert_fusion.13
  171.0 1.1 copy-done.9
  172.0 0.8 convolution_convert_fusion.14
  173.4 0.8 fusion.70
  174.2 14.2 %conditional.35 = (bf16[64,512]{1,0:T(8,128)(2,1)S(1)}) conditional(s32[]{:T(128)} %convert_element_type.266, () %tuple.123, (bf16[64,512]{1,0:T(8,128)(2,1)}, bf16[64,512]{1,0:T(8,128)(2,1)S(1)}, bf16[64,512]{1,0:T(8,128)(2,1)S(1)}, s32[2,2]{1,0:T(2,128)S(1)}, bf16[64,512]{1,0:T(8,128)(2,1)S(1)}, /*index=5*/bf16[64,512]{1,0:T(8,128)(2,1)S(1)}, ...), branch_computations={%region_43.44_spmd, %region_44.46_spmd} | conditional | flops 279245120 | bytes 30687596 | solution.py:87
  175.2 1.7 collective-permute-start.39
  176.9 2.4 %collective-permute-done.39 = bf16[1,64,512]{2,1,0:T(8,128)(2,1)S(1)} collective-permute-done((bf16[1,64,512]{2,1,0:T(8,128)(2,1)S(1)}, bf16[1,64,512]{2,1,0:T(8,128)(2,1)S(1)}, u32[]{:S(2)}, u32[]{:S(2)}) %collective-permute-start.39) | collective-permute-done | bytes 65568 | tf_op jit(solution)/shard_map/cond/branch_1_fun/ppermute | solution.py:34
  179.3 1.4 collective-permute-start.42
  180.8 1.0 collective-permute-start.41
  182.1 1.2 collective-permute-done.42
  183.2 1.4 collective-permute-done.41
  184.6 1.9 collective-permute-done.40
  186.7 1.7 fusion.74
  188.4 0.6 select_select_fusion
  (69 shorter events, 4.5 us)
Async XLA Ops:
  0.7 5.8 %copy-start.16 = (bf16[2,32,512]{2,1,0:T(8,128)(2,1)S(1)}, bf16[2,32,512]{2,1,0:T(8,128)(2,1)}, u32[]{:S(2)}) copy-start(bf16[2,32,512]{2,1,0:T(8,128)(2,1)} %param.45) | copy-start | bytes 196612
  0.8 5.8 %copy-start.17 = (s32[2,2]{1,0:T(2,128)S(1)}, s32[2,2]{1,0:T(2,128)}, u32[]{:S(2)}) copy-start(s32[2,2]{1,0:T(2,128)} %param.47) | copy-start | bytes 52
  6.6 42.4 %copy-start.18 = (s32[2,32]{1,0:T(2,128)S(1)}, s32[2,32]{1,0:T(2,128)}, u32[]{:S(2)}) copy-start(s32[2,32]{1,0:T(2,128)} %param.46) | copy-start | bytes 772
  8.8 40.2 %collective-permute-start.1 = (bf16[64,512]{1,0:T(8,128)(2,1)S(1)}, bf16[64,512]{1,0:T(8,128)(2,1)}, u32[]{:S(2)}, u32[]{:S(2)}) collective-permute-start(bf16[64,512]{1,0:T(8,128)(2,1)S(1)} %param.5), channel_id=1, source_target_pairs={{24,16},{16,24},{25,17},{17,25},{26,18},{18,26},{27,19},{19,27},{2... | collective-permute-start | bytes 196616 | tf_op jit(solution)/shard_map/cond/branch_1_fun/ppermute | solution.py:60
  52.4 96.3 %collective-permute-start.4 = (bf16[64,4096]{1,0:T(8,128)(2,1)S(1)}, bf16[64,4096]{1,0:T(8,128)(2,1)}, u32[]{:S(2)}, u32[]{:S(2)}) collective-permute-start(bf16[64,4096]{1,0:T(8,128)(2,1)S(1)} %param.17), channel_id=1, source_target_pairs={{16,24},{24,16},{17,25},{25,17},{18,26},{26,18},{19,27},{27,19},{2... | collective-permute-start | bytes 1572872 | tf_op jit(solution)/shard_map/cond/branch_1_fun/ppermute | solution.py:60
  148.7 4.7 %copy-start.8 = (bf16[4096,512]{1,0:T(8,128)(2,1)S(1)}, bf16[4096,512]{1,0:T(8,128)(2,1)}, u32[]{:S(2)}) copy-start(bf16[4096,512]{1,0:T(8,128)(2,1)} %get-tuple-element.201) | copy-start | bytes 12582916 | tf_op jit(solution)/shard_map/cond
  155.5 3.3 %collective-permute-start.6 = (bf16[64,512]{1,0:T(8,128)(2,1)S(1)}, bf16[64,512]{1,0:T(8,128)(2,1)}, u32[]{:S(2)}, u32[]{:S(2)}) collective-permute-start(bf16[64,512]{1,0:T(8,128)(2,1)S(1)} %param.31), channel_id=1, source_target_pairs={{16,24},{24,16},{17,25},{25,17},{18,26},{26,18},{19,27},{27,19},{2... | collective-permute-start | bytes 196616 | tf_op jit(solution)/shard_map/cond/branch_1_fun/ppermute | solution.py:60
  158.8 4.4 %collective-permute-start.35 = (bf16[1,64,512]{2,1,0:T(8,128)(2,1)}, bf16[1,64,512]{2,1,0:T(8,128)(2,1)S(1)}, u32[]{:S(2)}, u32[]{:S(2)}) collective-permute-start(bf16[1,64,512]{2,1,0:T(8,128)(2,1)} %bitcast.125), channel_id=1, source_target_pairs={{0,4},{1,5},{2,6},{3,7},{4,0},{5,1},{6,2},{7,3},{8,12},{9,13},{10,... | collective-permute-start | bytes 196616 | tf_op jit(solution)/shard_map/cond/branch_1_fun/ppermute | solution.py:34
  164.1 3.9 %collective-permute-start.38 = (bf16[2,1,64,512]{3,2,0,1:T(8,128)(2,1)S(1)}, bf16[2,1,64,512]{3,2,0,1:T(8,128)(2,1)S(1)}, u32[]{:S(2)}, u32[]{:S(2)}) collective-permute-start(bf16[2,1,64,512]{3,2,0,1:T(8,128)(2,1)S(1)} %pad_maximum_fusion.8), channel_id=1, source_target_pairs={{0,2},{1,3},{2,0},{3,1},{4,6},{5,7},{6,4},{7,5},{8,10},{9,11},{10,... | collective-permute-start | bytes 393224 | tf_op jit(solution)/shard_map/cond/branch_1_fun/ppermute | solution.py:34
  164.2 3.9 %collective-permute-start.37 = (bf16[2,1,64,512]{3,2,0,1:T(8,128)(2,1)S(1)}, bf16[2,1,64,512]{3,2,0,1:T(8,128)(2,1)S(1)}, u32[]{:S(2)}, u32[]{:S(2)}) collective-permute-start(bf16[2,1,64,512]{3,2,0,1:T(8,128)(2,1)S(1)} %pad_maximum_fusion.8), channel_id=1, source_target_pairs={{0,1},{1,0},{2,3},{3,2},{4,5},{5,4},{6,7},{7,6},{8,9},{9,8},{10,11... | collective-permute-start | bytes 393224 | tf_op jit(solution)/shard_map/cond/branch_1_fun/ppermute | solution.py:34
  164.6 4.9 %collective-permute-start.36 = (bf16[2,1,64,512]{3,2,0,1:T(8,128)(2,1)S(1)}, bf16[2,1,64,512]{3,2,0,1:T(8,128)(2,1)S(1)}, u32[]{:S(2)}, u32[]{:S(2)}) collective-permute-start(bf16[2,1,64,512]{3,2,0,1:T(8,128)(2,1)S(1)} %pad_maximum_fusion.8), channel_id=1, source_target_pairs={{0,3},{1,2},{2,1},{3,0},{4,7},{5,6},{6,5},{7,4},{8,11},{9,10},{10,... | collective-permute-start | bytes 393224 | tf_op jit(solution)/shard_map/cond/branch_1_fun/ppermute | solution.py:34
  166.8 3.3 %copy-start.3 = (bf16[4096,512]{1,0:T(8,128)(2,1)S(1)}, bf16[4096,512]{1,0:T(8,128)(2,1)}, u32[]{:S(2)}) copy-start(bf16[4096,512]{1,0:T(8,128)(2,1)} %get-tuple-element.227) | copy-start | bytes 12582916 | tf_op jit(solution)/shard_map/cond
  169.8 2.2 %copy-start.9 = (bf16[4096,512]{1,0:T(8,128)(2,1)S(1)}, bf16[4096,512]{1,0:T(8,128)(2,1)}, u32[]{:S(2)}) copy-start(bf16[4096,512]{1,0:T(8,128)(2,1)} %get-tuple-element.226) | copy-start | bytes 12582916 | tf_op jit(solution)/shard_map/cond
  170.1 3.3 %copy-start.11 = (bf16[4096,512]{1,0:T(8,128)(2,1)S(1)}, bf16[4096,512]{1,0:T(8,128)(2,1)}, u32[]{:S(2)}) copy-start(bf16[4096,512]{1,0:T(8,128)(2,1)} %get-tuple-element.225) | copy-start | bytes 12582916 | tf_op jit(solution)/shard_map/cond
  175.2 4.1 %collective-permute-start.39 = (bf16[1,64,512]{2,1,0:T(8,128)(2,1)S(1)}, bf16[1,64,512]{2,1,0:T(8,128)(2,1)S(1)}, u32[]{:S(2)}, u32[]{:S(2)}) collective-permute-start(bf16[1,64,512]{2,1,0:T(8,128)(2,1)S(1)} %reshape.241), channel_id=1, source_target_pairs={{0,4},{1,5},{2,6},{3,7},{4,0},{5,1},{6,2},{7,3},{8,12},{9,13},{10,... | collective-permute-start | bytes 196616 | tf_op jit(solution)/shard_map/cond/branch_1_fun/ppermute | solution.py:34
  179.3 3.9 %collective-permute-start.42 = (bf16[2,1,64,512]{3,2,0,1:T(8,128)(2,1)S(1)}, bf16[2,1,64,512]{3,2,0,1:T(8,128)(2,1)S(1)}, u32[]{:S(2)}, u32[]{:S(2)}) collective-permute-start(bf16[2,1,64,512]{3,2,0,1:T(8,128)(2,1)S(1)} %fusion.84), channel_id=1, source_target_pairs={{0,2},{1,3},{2,0},{3,1},{4,6},{5,7},{6,4},{7,5},{8,10},{9,11},{10,... | collective-permute-start | bytes 393224 | tf_op jit(solution)/shard_map/cond/branch_1_fun/ppermute | solution.py:34
  180.8 3.8 %collective-permute-start.41 = (bf16[2,1,64,512]{3,2,0,1:T(8,128)(2,1)S(1)}, bf16[2,1,64,512]{3,2,0,1:T(8,128)(2,1)S(1)}, u32[]{:S(2)}, u32[]{:S(2)}) collective-permute-start(bf16[2,1,64,512]{3,2,0,1:T(8,128)(2,1)S(1)} %fusion.84), channel_id=1, source_target_pairs={{0,1},{1,0},{2,3},{3,2},{4,5},{5,4},{6,7},{7,6},{8,9},{9,8},{10,11... | collective-permute-start | bytes 393224 | tf_op jit(solution)/shard_map/cond/branch_1_fun/ppermute | solution.py:34
  181.7 4.7 %collective-permute-start.40 = (bf16[2,1,64,512]{3,2,0,1:T(8,128)(2,1)S(1)}, bf16[2,1,64,512]{3,2,0,1:T(8,128)(2,1)S(1)}, u32[]{:S(2)}, u32[]{:S(2)}) collective-permute-start(bf16[2,1,64,512]{3,2,0,1:T(8,128)(2,1)S(1)} %fusion.84), channel_id=1, source_target_pairs={{0,3},{1,2},{2,1},{3,0},{4,7},{5,6},{6,5},{7,4},{8,11},{9,10},{10,... | collective-permute-start | bytes 393224 | tf_op jit(solution)/shard_map/cond/branch_1_fun/ppermute | solution.py:34
  182.1 4.7 %copy-start.15 = (bf16[4096,512]{1,0:T(8,128)(2,1)S(1)}, bf16[4096,512]{1,0:T(8,128)(2,1)}, u32[]{:S(2)}) copy-start(bf16[4096,512]{1,0:T(8,128)(2,1)} %get-tuple-element.235) | copy-start | bytes 12582916 | tf_op jit(solution)/shard_map/cond

commit v2 on v1

--- a/solution.py
+++ b/solution.py
@@ -53,14 +53,11 @@
 
 
 def exchange(block, axis, first, second):
-    index = lax.axis_index(axis)
+    rest = [i for i in range(lax.axis_size(axis)) if i not in (first, second)]
     route = [(first, second), (second, first)]
-    return lax.cond(
-        (index == first) | (index == second),
-        lambda rows: lax.ppermute(rows, axis, route),
-        lambda rows: rows,
-        block,
-    )
+    for i in range(0, len(rest) - 1, 2):
+        route += [(rest[i], rest[i + 1]), (rest[i + 1], rest[i])]
+    return lax.ppermute(block, axis, route)
 
 
 def local(patches, table_ids, lengths, embed_table, norm_gain, w_query, w_key, w_value, w_out):
@@ -76,7 +73,6 @@
     key_weight = w_key[0]
     value_weight = w_value[0]
     out_weight = w_out[0]
-    gain_row = norm_gain[0].astype(jnp.float32)
     total_rows = micro_count * row_count
     vocab_local = embed_table.shape[0]
 
@@ -97,7 +93,7 @@
     def normalise(full):
         values_f = full.astype(jnp.float32)
         inverse = lax.rsqrt(jnp.mean(values_f * values_f, axis=-1, keepdims=True) + epsilon)
-        return (values_f * inverse * gain_row).astype(jnp.bfloat16)
+        return (values_f * inverse * norm_gain[0].astype(jnp.float32)).astype(jnp.bfloat16)
 
     def project(normed, weight):
         return jnp.dot(normed, weight, preferred_element_type=jnp.float32)
@@ -162,35 +158,51 @@
     def after(value, *earlier):
         return lax.optimization_barrier((value,) + earlier)[0]
 
+    def member(*indices):
+        taken = section_index == indices[0]
+        for index in indices[1:]:
+            taken = taken | (section_index == index)
+        return taken
+
+    def look_up_and_add():
+        found = look_up()
+        others = list(range(1, section_count))
+        total = found
+        for shift in range(1, len(others)):
+            route = [(s, others[(i + shift) % len(others)]) for i, s in enumerate(others)]
+            total = total + lax.ppermute(found, "section", route)
+        return total
+
+    def embed(found):
+        own = lax.cond(section_index == 0, look_up, lambda: found)
+        sent = lax.ppermute(own, "section", [(0, half), (half, 0)])
+        embedded = own + sent
+        return (embedded, *only([half], table_rows, (embedded,), (part, part, part)))
+
     stream = patches.reshape(total_rows, width_local)
     (updated,) = only([0], encode, (stream,), (part,))
     result = updated
-    rows_found = lax.cond(section_index != 0, look_up, lambda: jnp.zeros(*part))
-    for index in range(1, section_count):
-        if index != half:
-            sent = exchange(rows_found, "section", index, half)
-            rows_found = jnp.where(section_index == half, rows_found + sent, rows_found)
-    stream = exchange(updated, "section", 0, 1)
-    rows_found, stream = lax.optimization_barrier((rows_found, stream))
-    own_found = lax.cond(section_index == 0, look_up, lambda: rows_found)
-    sent = exchange(own_found, "section", 0, half)
-    embedded = own_found + sent
-    table = only([half], table_rows, (embedded,), (part, part, part))
-    for index in range(1, half):
-        (updated,) = only([index], encode, (stream,), (part,))
-        result = jnp.where(section_index == index, updated, result)
-        stream = exchange(updated, "section", index, index + 1)
+    found = lax.cond(section_index != 0, look_up_and_add, lambda: jnp.zeros(*part))
+    table = None
+    for index in range(half):
+        if index:
+            (updated,) = only([index], encode, (stream,), (part,))
+            result = jnp.where(section_index == index, updated, result)
+        earlier = (found,) if table is None else table
+        stream = exchange(after(updated, *earlier), "section", index, index + 1)
+        if table is None:
+            table = only([0, half], embed, (after(found, stream),), (part,) * 4)
+    embedded, *table = table
 
     (memory,) = only([half], lambda block: (gathered(block),), (stream,), (whole,))
     stream = embedded
     for index in range(half, section_count):
-        if index > half:
-            memory_next = exchange(memory, "section", index - 1, index)
-            memory = jnp.where(section_index == index, memory_next, memory)
         pair = only([index], memory_rows, (memory,), (part, part))
         if index > half:
             stream = exchange(after(stream, *pair), "section", index - 1, index)
             table = only([index], table_rows, (stream,), (part, part, part))
+        if index + 1 < section_count:
+            memory = exchange(memory, "section", index, index + 1)
         (updated,) = only([index], decode, (stream, *pair, *table), (part,))
         result = jnp.where(section_index == index, updated, result)
         stream = updated

time: 190 us -> 145 us (0.76)
  starting transfers between devices: 145 us -> 103 us
  other arithmetic: 7.81 us -> 1.8 us
  waiting for transfers between devices: 16 us -> 20.2 us
  matrix products: 14.8 us -> 12.9 us
    ppermute x3 -> x6, starting transfers between devices: 136 us -> 93.4 us  [the longest x4 88.9 us: exchange(): return lax.ppermute(block, axis, route)]
    ppermute x3 -> x6, waiting for transfers between devices: 4.01 us -> 8.41 us  [the longest x4 5.44 us: exchange(): return lax.ppermute(block, axis, route)]
    another operation x10 -> x11, local copies, waits for them, and re-layouts: 0.2 us -> 3.54 us
    cond x14 -> x10, local copies, waits for them, and re-layouts: 4.07 us -> 1.58 us
    dot_general x6, matrix products: 9.39 us -> 7.46 us  [project(): return jnp.dot(normed, weight, preferred_element_type=jnp.float32)]
  transfers between devices with their start and end apart: 11 -> 14, of which waited for: 11 -> 11; matrix products, arithmetic and copies ran while one was open for 0% -> 0% of each run, Pallas kernels for 0% -> 0%
where the time goes in v2:
time: 145 us
  starting transfers between devices  103 us (71%)
  waiting for transfers between devices  20.2 us (14%)
  matrix products  12.9 us (9%)
  local copies, waits for them, and re-layouts  6.26 us (4%)
  other arithmetic  1.8 us (1%)
    ppermute x4, starting transfers between devices, exchange(): return lax.ppermute(block, axis, route)  88.9 us
    ppermute x8, waiting for transfers between devices, gather_rows(): pieces[mask] = lax.ppermute(held, axis, route)  11.8 us
    ppermute x8, starting transfers between devices, gather_rows(): pieces[mask] = lax.ppermute(held, axis, route)  9.44 us
    dot_general x6, matrix products, project(): return jnp.dot(normed, weight, preferred_element_type=jnp.float32)  7.46 us
    ppermute x4, waiting for transfers between devices, exchange(): return lax.ppermute(block, axis, route)  5.44 us
    dot_general x1, matrix products, look_up(): jnp.dot(one_hot, embed_table, preferred_element_type=jnp.float32)  4.99 us
    ppermute x2, starting transfers between devices, look_up_and_add(): total = total + lax.ppermute(found, 'section', route)  4.51 us
    another operation x11, local copies, waits for them, and re-layouts  3.54 us
  transfers between devices with their start and end apart: 14, of which 11 were waited for; matrix products, arithmetic and copies ran while one was open for 0% of the time, Pallas kernels for 0%

profile of v2, /device:TPU:3, one launch (start us, length us, event | category | flops | bytes accessed | tf_op | source)
XLA Modules:
  0.0 144.6 jit_solution(1849001368489523145)
XLA Ops:
  0.0 0.7 copy-done.17
  0.7 12.6 %conditional.12 = (bf16[64,512]{1,0:T(8,128)(2,1)S(1)}) conditional(s32[]{:T(128)} %convert_element_type.267, () %tuple.94, (s32[]{:T(128)}, s32[2,32]{1,0:T(2,128)S(1)}, bf16[8192,512]{1,0:T(8,128)(2,1)}) %tuple.218), branch_computations={%region_4.5_spmd, %region_5.6_spmd} | conditional | flops 537493568 | bytes 9241960 | solution.py:185
  0.8 5.0 %fusion.13 = bf16[64,512]{1,0:T(8,128)(2,1)S(1)} fusion(bf16[8192,512]{1,0:T(8,128)(2,1)} %get-tuple-element.164, s32[64]{0:T(128)S(1)} %sub.22), kind=kOutput, calls=%fused_computation.49 | convolution fusion | flops 537427968 | bytes 8454400 | tf_op jit(solution)/shard_map/cond/branch_1_fun/dot_general | solution.py:89
  5.8 1.9 %collective-permute-start.12 = (bf16[64,512]{1,0:T(8,128)(2,1)S(1)}, bf16[64,512]{1,0:T(8,128)(2,1)S(1)}, u32[]{:S(2)}, u32[]{:S(2)}) collective-permute-start(bf16[64,512]{1,0:T(8,128)(2,1)S(1)} %fusion.13), channel_id=1, source_target_pairs={{8,16},{16,24},{24,8},{9,17},{17,25},{25,9},{10,18},{18,26},{26,10... | collective-permute-start | bytes 196616 | tf_op jit(solution)/shard_map/cond/branch_1_fun/ppermute | solution.py:173
  7.7 2.6 %collective-permute-start.13 = (bf16[64,512]{1,0:T(8,128)(2,1)S(1)}, bf16[64,512]{1,0:T(8,128)(2,1)S(1)}, u32[]{:S(2)}, u32[]{:S(2)}) collective-permute-start(bf16[64,512]{1,0:T(8,128)(2,1)S(1)} %fusion.13), channel_id=1, source_target_pairs={{8,24},{16,8},{24,16},{9,25},{17,9},{25,17},{10,26},{18,10},{26,18... | collective-permute-start | bytes 196616 | tf_op jit(solution)/shard_map/cond/branch_1_fun/ppermute | solution.py:173
  10.3 3.0 %collective-permute-done.13 = bf16[64,512]{1,0:T(8,128)(2,1)S(1)} collective-permute-done((bf16[64,512]{1,0:T(8,128)(2,1)S(1)}, bf16[64,512]{1,0:T(8,128)(2,1)S(1)}, u32[]{:S(2)}, u32[]{:S(2)}) %collective-permute-start.13) | collective-permute-done | bytes 65568 | tf_op jit(solution)/shard_map/cond/branch_1_fun/ppermute | solution.py:173
  13.3 0.7 collective-permute-start.39
  14.0 0.9 collective-permute-done.39
  14.9 2.5 %conditional.14 = (bf16[64,512]{1,0:T(8,128)(2,1)}, bf16[64,512]{1,0:T(8,128)(2,1)}, bf16[64,512]{1,0:T(8,128)(2,1)}, bf16[64,512]{1,0:T(8,128)(2,1)}) conditional(s32[]{:T(128)} %convert_element_type.266, () %tuple.93, (s32[]{:T(128)}, bf16[64,512]{1,0:T(8,128)(2,1)S(1)}, s32[2,32]{1,0:T(2,128)S(1)}, bf16[8192,512]{1,0:T(8,128)(2,1)}, ...), branch_computations={%region_10.11_spmd, %region_11.17_spmd} | conditional | flops 1347031168 | bytes 82815776 | solution.py:83
  14.9 0.6 broadcast.155
  15.5 0.6 broadcast.155.clone
  16.2 0.6 broadcast.155.clone.1
  16.8 0.6 broadcast.155.clone.2
  17.6 36.3 %collective-permute-start.40 = (bf16[64,512]{1,0:T(8,128)(2,1)S(1)}, bf16[64,512]{1,0:T(8,128)(2,1)S(1)}, u32[]{:S(2)}, u32[]{:S(2)}) collective-permute-start(bf16[64,512]{1,0:T(8,128)(2,1)S(1)} %get-tuple-element.439), channel_id=1, source_target_pairs={{8,16},{16,8},{0,24},{24,0},{9,17},{17,9},{1,25},{25,1},{10,18},{1... | collective-permute-start | bytes 196616 | tf_op jit(solution)/shard_map/ppermute | solution.py:60
  53.9 2.0 %collective-permute-done.40 = bf16[64,512]{1,0:T(8,128)(2,1)S(1)} collective-permute-done((bf16[64,512]{1,0:T(8,128)(2,1)S(1)}, bf16[64,512]{1,0:T(8,128)(2,1)S(1)}, u32[]{:S(2)}, u32[]{:S(2)}) %collective-permute-start.40) | collective-permute-done | bytes 65568 | tf_op jit(solution)/shard_map/ppermute | solution.py:60
  55.9 0.9 conditional.16
  55.9 0.9 broadcast.160
  56.8 32.8 %collective-permute-start.41 = (bf16[64,4096]{1,0:T(8,128)(2,1)}, bf16[64,4096]{1,0:T(8,128)(2,1)S(1)}, u32[]{:S(2)}, u32[]{:S(2)}) collective-permute-start(bf16[64,4096]{1,0:T(8,128)(2,1)} %get-tuple-element.440), channel_id=1, source_target_pairs={{16,24},{24,16},{0,8},{8,0},{17,25},{25,17},{1,9},{9,1},{18,26},{2... | collective-permute-start | bytes 1572872 | tf_op jit(solution)/shard_map/ppermute | solution.py:60
  89.6 1.7 %collective-permute-done.41 = bf16[64,4096]{1,0:T(8,128)(2,1)S(1)} collective-permute-done((bf16[64,4096]{1,0:T(8,128)(2,1)}, bf16[64,4096]{1,0:T(8,128)(2,1)S(1)}, u32[]{:S(2)}, u32[]{:S(2)}) %collective-permute-start.41) | collective-permute-done | bytes 524320 | tf_op jit(solution)/shard_map/ppermute | solution.py:60
  91.3 4.4 %conditional.19 = (bf16[64,512]{1,0:T(8,128)(2,1)S(1)}, bf16[64,512]{1,0:T(8,128)(2,1)S(1)}) conditional(s32[]{:T(128)} %convert_element_type.264, () %tuple.108, (bf16[64,4096]{1,0:T(8,128)(2,1)S(1)}, bf16[1,4096]{1,0:T(2,128)(2,1)S(1)}, bf16[4096,512]{1,0:T(8,128)(2,1)}, bf16[4096,512]{1,0:T(8,128)(2,1)}) %tuple.213), branch_computations={%region_19.20_spmd, %region_20.22_spmd} | conditional | flops 539824192 | bytes 26928428 | solution.py:83
  91.6 3.2 %convolution_convert_fusion.8 = bf16[64,512]{1,0:T(8,128)(2,1)S(1)} fusion(bf16[4096,512]{1,0:T(8,128)(2,1)} %get-tuple-element.194, bf16[64,4096]{1,0:T(8,128)(2,1)S(1)} %get-tuple-element.191, f32[4096]{0:T(1024)S(1)} %bitcast.522, f32[64]{0:T(128)S(1)} %add_rsqrt_fusion.3), kind=kOutput, calls=%fused_computation.139 | convolution fusion | flops 269516800 | bytes 4800768 | tf_op jit(solution)/shard_map/cond/branch_1_fun/dot_general | solution.py:99
  94.8 0.9 convolution_convert_fusion.9
  95.7 19.1 %collective-permute-start.42 = (bf16[64,512]{1,0:T(8,128)(2,1)S(1)}, bf16[64,512]{1,0:T(8,128)(2,1)S(1)}, u32[]{:S(2)}, u32[]{:S(2)}) collective-permute-start(bf16[64,512]{1,0:T(8,128)(2,1)S(1)} %get-tuple-element.441), channel_id=1, source_target_pairs={{16,24},{24,16},{0,8},{8,0},{17,25},{25,17},{1,9},{9,1},{18,26},{2... | collective-permute-start | bytes 196616 | tf_op jit(solution)/shard_map/ppermute | solution.py:60
  114.9 0.9 collective-permute-done.42
  115.8 15.4 %conditional.20 = (bf16[64,512]{1,0:T(8,128)(2,1)S(1)}, bf16[64,512]{1,0:T(8,128)(2,1)S(1)}, bf16[64,512]{1,0:T(8,128)(2,1)S(1)}) conditional(s32[]{:T(128)} %convert_element_type.264, () %tuple.111, (bf16[64,512]{1,0:T(8,128)(2,1)S(1)}, bf16[1,4096]{1,0:T(2,128)(2,1)S(1)}, bf16[4096,512]{1,0:T(8,128)(2,1)}, bf16[4096,512]{1,0:T(8,128)(2,1)}, ...), branch_computations={%region_28.29_spmd, %region_29.31_spmd} | conditional | flops 809570368 | bytes 73901416 | solution.py:83
  115.8 1.9 %collective-permute-start.31 = (bf16[1,64,512]{2,1,0:T(8,128)(2,1)S(1)}, bf16[1,64,512]{2,1,0:T(8,128)(2,1)S(1)}, u32[]{:S(2)}, u32[]{:S(2)}) collective-permute-start(bf16[1,64,512]{2,1,0:T(8,128)(2,1)S(1)} %bitcast.519), channel_id=1, source_target_pairs={{0,4},{1,5},{2,6},{3,7},{4,0},{5,1},{6,2},{7,3},{8,12},{9,13},{10,... | collective-permute-start | bytes 196616 | tf_op jit(solution)/shard_map/cond/branch_1_fun/ppermute | solution.py:34
  117.7 2.8 %collective-permute-done.31 = bf16[1,64,512]{2,1,0:T(8,128)(2,1)S(1)} collective-permute-done((bf16[1,64,512]{2,1,0:T(8,128)(2,1)S(1)}, bf16[1,64,512]{2,1,0:T(8,128)(2,1)S(1)}, u32[]{:S(2)}, u32[]{:S(2)}) %collective-permute-start.31) | collective-permute-done | bytes 65568 | tf_op jit(solution)/shard_map/cond/branch_1_fun/ppermute | solution.py:34
  120.5 0.7 collective-permute-start.32
  121.2 0.6 collective-permute-start.33
  121.8 1.4 collective-permute-start.34
  123.3 2.1 %collective-permute-done.32 = bf16[2,1,64,512]{3,2,0,1:T(8,128)(2,1)S(1)} collective-permute-done((bf16[2,1,64,512]{3,2,0,1:T(8,128)(2,1)S(1)}, bf16[2,1,64,512]{3,2,0,1:T(8,128)(2,1)S(1)}, u32[]{:S(2)}, u32[]{:S(2)}) %collective-permute-start.32) | collective-permute-done | bytes 131104 | tf_op jit(solution)/shard_map/cond/branch_1_fun/ppermute | solution.py:34
  125.4 1.0 collective-permute-done.33
  127.1 0.8 convolution_convert_fusion.13
  127.9 1.1 copy-done.3
  129.0 0.8 convolution_convert_fusion.14
  129.8 0.5 copy-done.9
  130.3 0.8 fusion.70
  131.2 12.8 %conditional.21 = (bf16[64,512]{1,0:T(8,128)(2,1)S(1)}) conditional(s32[]{:T(128)} %convert_element_type.264, () %tuple.91, (bf16[64,512]{1,0:T(8,128)(2,1)S(1)}, bf16[64,512]{1,0:T(8,128)(2,1)S(1)}, bf16[64,512]{1,0:T(8,128)(2,1)S(1)}, s32[2,2]{1,0:T(2,128)S(1)}, bf16[64,512]{1,0:T(8,128)(2,1)S(1)}, /*index=5*/bf16[64,512]{1,0:T(8,128)(2,1)S(1)}, ...), branch_computations={%region_31.32_spmd, %region_32.34_spmd} | conditional | flops 279245120 | bytes 30687596 | solution.py:83
  131.9 0.2 fusion.75
  132.2 2.1 %collective-permute-start.35 = (bf16[1,64,512]{2,1,0:T(8,128)(2,1)S(1)}, bf16[1,64,512]{2,1,0:T(8,128)(2,1)S(1)}, u32[]{:S(2)}, u32[]{:S(2)}) collective-permute-start(bf16[1,64,512]{2,1,0:T(8,128)(2,1)S(1)} %reshape.233), channel_id=1, source_target_pairs={{0,4},{1,5},{2,6},{3,7},{4,0},{5,1},{6,2},{7,3},{8,12},{9,13},{10,... | collective-permute-start | bytes 196616 | tf_op jit(solution)/shard_map/cond/branch_1_fun/ppermute | solution.py:34
  134.3 2.7 %collective-permute-done.35 = bf16[1,64,512]{2,1,0:T(8,128)(2,1)S(1)} collective-permute-done((bf16[1,64,512]{2,1,0:T(8,128)(2,1)S(1)}, bf16[1,64,512]{2,1,0:T(8,128)(2,1)S(1)}, u32[]{:S(2)}, u32[]{:S(2)}) %collective-permute-start.35) | collective-permute-done | bytes 65568 | tf_op jit(solution)/shard_map/cond/branch_1_fun/ppermute | solution.py:34
  137.0 0.6 collective-permute-start.36
  137.6 0.7 collective-permute-start.37
  138.3 1.4 collective-permute-start.38
  139.7 2.2 %collective-permute-done.36 = bf16[2,1,64,512]{3,2,0,1:T(8,128)(2,1)S(1)} collective-permute-done((bf16[2,1,64,512]{3,2,0,1:T(8,128)(2,1)S(1)}, bf16[2,1,64,512]{3,2,0,1:T(8,128)(2,1)S(1)}, u32[]{:S(2)}, u32[]{:S(2)}) %collective-permute-start.36) | collective-permute-done | bytes 131104 | tf_op jit(solution)/shard_map/cond/branch_1_fun/ppermute | solution.py:34
  141.9 0.9 collective-permute-done.37
  143.1 0.8 fusion.74
  143.9 0.6 select_select_fusion
  (63 shorter events, 2.2 us)
Async XLA Ops:
  0.0 0.7 copy-start.17
  0.7 14.2 %copy-start.14 = (bf16[1,4096]{1,0:T(2,128)(2,1)S(1)}, bf16[1,4096]{1,0:T(2,128)(2,1)}, u32[]{:S(2)}) copy-start(bf16[1,4096]{1,0:T(2,128)(2,1)} %param.37) | copy-start | bytes 24580
  5.8 4.5 %collective-permute-start.12 = (bf16[64,512]{1,0:T(8,128)(2,1)S(1)}, bf16[64,512]{1,0:T(8,128)(2,1)S(1)}, u32[]{:S(2)}, u32[]{:S(2)}) collective-permute-start(bf16[64,512]{1,0:T(8,128)(2,1)S(1)} %fusion.13), channel_id=1, source_target_pairs={{8,16},{16,24},{24,8},{9,17},{17,25},{25,9},{10,18},{18,26},{26,10... | collective-permute-start | bytes 196616 | tf_op jit(solution)/shard_map/cond/branch_1_fun/ppermute | solution.py:173
  7.7 5.6 %collective-permute-start.13 = (bf16[64,512]{1,0:T(8,128)(2,1)S(1)}, bf16[64,512]{1,0:T(8,128)(2,1)S(1)}, u32[]{:S(2)}, u32[]{:S(2)}) collective-permute-start(bf16[64,512]{1,0:T(8,128)(2,1)S(1)} %fusion.13), channel_id=1, source_target_pairs={{8,24},{16,8},{24,16},{9,25},{17,9},{25,17},{10,26},{18,10},{26,18... | collective-permute-start | bytes 196616 | tf_op jit(solution)/shard_map/cond/branch_1_fun/ppermute | solution.py:173
  13.3 1.6 %collective-permute-start.39 = (bf16[64,512]{1,0:T(8,128)(2,1)S(1)}, bf16[64,512]{1,0:T(8,128)(2,1)S(1)}, u32[]{:S(2)}, u32[]{:S(2)}) collective-permute-start(bf16[64,512]{1,0:T(8,128)(2,1)S(1)} %get-tuple-element.438), channel_id=1, source_target_pairs={{0,8},{8,0},{16,24},{24,16},{1,9},{9,1},{17,25},{25,17},{2,10},{10... | collective-permute-start | bytes 196616 | tf_op jit(solution)/shard_map/ppermute | solution.py:60
  14.9 2.5 %copy-start.16 = (s32[2,2]{1,0:T(2,128)S(1)}, s32[2,2]{1,0:T(2,128)}, u32[]{:S(2)}) copy-start(s32[2,2]{1,0:T(2,128)} %param.35) | copy-start | bytes 52
  17.6 38.3 %collective-permute-start.40 = (bf16[64,512]{1,0:T(8,128)(2,1)S(1)}, bf16[64,512]{1,0:T(8,128)(2,1)S(1)}, u32[]{:S(2)}, u32[]{:S(2)}) collective-permute-start(bf16[64,512]{1,0:T(8,128)(2,1)S(1)} %get-tuple-element.439), channel_id=1, source_target_pairs={{8,16},{16,8},{0,24},{24,0},{9,17},{17,9},{1,25},{25,1},{10,18},{1... | collective-permute-start | bytes 196616 | tf_op jit(solution)/shard_map/ppermute | solution.py:60
  56.8 34.5 %collective-permute-start.41 = (bf16[64,4096]{1,0:T(8,128)(2,1)}, bf16[64,4096]{1,0:T(8,128)(2,1)S(1)}, u32[]{:S(2)}, u32[]{:S(2)}) collective-permute-start(bf16[64,4096]{1,0:T(8,128)(2,1)} %get-tuple-element.440), channel_id=1, source_target_pairs={{16,24},{24,16},{0,8},{8,0},{17,25},{25,17},{1,9},{9,1},{18,26},{2... | collective-permute-start | bytes 1572872 | tf_op jit(solution)/shard_map/ppermute | solution.py:60
  91.3 3.5 %copy-start.2 = (bf16[4096,512]{1,0:T(8,128)(2,1)S(1)}, bf16[4096,512]{1,0:T(8,128)(2,1)}, u32[]{:S(2)}) copy-start(bf16[4096,512]{1,0:T(8,128)(2,1)} %get-tuple-element.193) | copy-start | bytes 12582916 | tf_op jit(solution)/shard_map/cond
  95.7 20.0 %collective-permute-start.42 = (bf16[64,512]{1,0:T(8,128)(2,1)S(1)}, bf16[64,512]{1,0:T(8,128)(2,1)S(1)}, u32[]{:S(2)}, u32[]{:S(2)}) collective-permute-start(bf16[64,512]{1,0:T(8,128)(2,1)S(1)} %get-tuple-element.441), channel_id=1, source_target_pairs={{16,24},{24,16},{0,8},{8,0},{17,25},{25,17},{1,9},{9,1},{18,26},{2... | collective-permute-start | bytes 196616 | tf_op jit(solution)/shard_map/ppermute | solution.py:60
  115.8 4.7 %collective-permute-start.31 = (bf16[1,64,512]{2,1,0:T(8,128)(2,1)S(1)}, bf16[1,64,512]{2,1,0:T(8,128)(2,1)S(1)}, u32[]{:S(2)}, u32[]{:S(2)}) collective-permute-start(bf16[1,64,512]{2,1,0:T(8,128)(2,1)S(1)} %bitcast.519), channel_id=1, source_target_pairs={{0,4},{1,5},{2,6},{3,7},{4,0},{5,1},{6,2},{7,3},{8,12},{9,13},{10,... | collective-permute-start | bytes 196616 | tf_op jit(solution)/shard_map/cond/branch_1_fun/ppermute | solution.py:34
  120.5 4.9 %collective-permute-start.32 = (bf16[2,1,64,512]{3,2,0,1:T(8,128)(2,1)S(1)}, bf16[2,1,64,512]{3,2,0,1:T(8,128)(2,1)S(1)}, u32[]{:S(2)}, u32[]{:S(2)}) collective-permute-start(bf16[2,1,64,512]{3,2,0,1:T(8,128)(2,1)S(1)} %pad_maximum_fusion.8), channel_id=1, source_target_pairs={{0,3},{1,2},{2,1},{3,0},{4,7},{5,6},{6,5},{7,4},{8,11},{9,10},{10,... | collective-permute-start | bytes 393224 | tf_op jit(solution)/shard_map/cond/branch_1_fun/ppermute | solution.py:34
  121.2 5.2 %collective-permute-start.33 = (bf16[2,1,64,512]{3,2,0,1:T(8,128)(2,1)S(1)}, bf16[2,1,64,512]{3,2,0,1:T(8,128)(2,1)S(1)}, u32[]{:S(2)}, u32[]{:S(2)}) collective-permute-start(bf16[2,1,64,512]{3,2,0,1:T(8,128)(2,1)S(1)} %pad_maximum_fusion.8), channel_id=1, source_target_pairs={{0,1},{1,0},{2,3},{3,2},{4,5},{5,4},{6,7},{7,6},{8,9},{9,8},{10,11... | collective-permute-start | bytes 393224 | tf_op jit(solution)/shard_map/cond/branch_1_fun/ppermute | solution.py:34
  121.8 4.6 %collective-permute-start.34 = (bf16[2,1,64,512]{3,2,0,1:T(8,128)(2,1)S(1)}, bf16[2,1,64,512]{3,2,0,1:T(8,128)(2,1)S(1)}, u32[]{:S(2)}, u32[]{:S(2)}) collective-permute-start(bf16[2,1,64,512]{3,2,0,1:T(8,128)(2,1)S(1)} %pad_maximum_fusion.8), channel_id=1, source_target_pairs={{0,2},{1,3},{2,0},{3,1},{4,6},{5,7},{6,4},{7,5},{8,10},{9,11},{10,... | collective-permute-start | bytes 393224 | tf_op jit(solution)/shard_map/cond/branch_1_fun/ppermute | solution.py:34
  123.2 3.8 %copy-start.5 = (bf16[4096,512]{1,0:T(8,128)(2,1)S(1)}, bf16[4096,512]{1,0:T(8,128)(2,1)}, u32[]{:S(2)}) copy-start(bf16[4096,512]{1,0:T(8,128)(2,1)} %get-tuple-element.211) | copy-start | bytes 12582916 | tf_op jit(solution)/shard_map/cond
  126.8 2.2 %copy-start.3 = (bf16[4096,512]{1,0:T(8,128)(2,1)S(1)}, bf16[4096,512]{1,0:T(8,128)(2,1)}, u32[]{:S(2)}) copy-start(bf16[4096,512]{1,0:T(8,128)(2,1)} %get-tuple-element.210) | copy-start | bytes 12582916 | tf_op jit(solution)/shard_map/cond
  127.1 3.3 %copy-start.9 = (bf16[4096,512]{1,0:T(8,128)(2,1)S(1)}, bf16[4096,512]{1,0:T(8,128)(2,1)}, u32[]{:S(2)}) copy-start(bf16[4096,512]{1,0:T(8,128)(2,1)} %get-tuple-element.209) | copy-start | bytes 12582916 | tf_op jit(solution)/shard_map/cond
  132.2 4.8 %collective-permute-start.35 = (bf16[1,64,512]{2,1,0:T(8,128)(2,1)S(1)}, bf16[1,64,512]{2,1,0:T(8,128)(2,1)S(1)}, u32[]{:S(2)}, u32[]{:S(2)}) collective-permute-start(bf16[1,64,512]{2,1,0:T(8,128)(2,1)S(1)} %reshape.233), channel_id=1, source_target_pairs={{0,4},{1,5},{2,6},{3,7},{4,0},{5,1},{6,2},{7,3},{8,12},{9,13},{10,... | collective-permute-start | bytes 196616 | tf_op jit(solution)/shard_map/cond/branch_1_fun/ppermute | solution.py:34
  137.0 4.9 %collective-permute-start.36 = (bf16[2,1,64,512]{3,2,0,1:T(8,128)(2,1)S(1)}, bf16[2,1,64,512]{3,2,0,1:T(8,128)(2,1)S(1)}, u32[]{:S(2)}, u32[]{:S(2)}) collective-permute-start(bf16[2,1,64,512]{3,2,0,1:T(8,128)(2,1)S(1)} %fusion.84), channel_id=1, source_target_pairs={{0,3},{1,2},{2,1},{3,0},{4,7},{5,6},{6,5},{7,4},{8,11},{9,10},{10,... | collective-permute-start | bytes 393224 | tf_op jit(solution)/shard_map/cond/branch_1_fun/ppermute | solution.py:34
  137.6 5.2 %collective-permute-start.37 = (bf16[2,1,64,512]{3,2,0,1:T(8,128)(2,1)S(1)}, bf16[2,1,64,512]{3,2,0,1:T(8,128)(2,1)S(1)}, u32[]{:S(2)}, u32[]{:S(2)}) collective-permute-start(bf16[2,1,64,512]{3,2,0,1:T(8,128)(2,1)S(1)} %fusion.84), channel_id=1, source_target_pairs={{0,1},{1,0},{2,3},{3,2},{4,5},{5,4},{6,7},{7,6},{8,9},{9,8},{10,11... | collective-permute-start | bytes 393224 | tf_op jit(solution)/shard_map/cond/branch_1_fun/ppermute | solution.py:34
  138.3 4.5 %collective-permute-start.38 = (bf16[2,1,64,512]{3,2,0,1:T(8,128)(2,1)S(1)}, bf16[2,1,64,512]{3,2,0,1:T(8,128)(2,1)S(1)}, u32[]{:S(2)}, u32[]{:S(2)}) collective-permute-start(bf16[2,1,64,512]{3,2,0,1:T(8,128)(2,1)S(1)} %fusion.84), channel_id=1, source_target_pairs={{0,2},{1,3},{2,0},{3,1},{4,6},{5,7},{6,4},{7,5},{8,10},{9,11},{10,... | collective-permute-start | bytes 393224 | tf_op jit(solution)/shard_map/cond/branch_1_fun/ppermute | solution.py:34
  139.7 3.4 %copy-start.13 = (bf16[4096,512]{1,0:T(8,128)(2,1)S(1)}, bf16[4096,512]{1,0:T(8,128)(2,1)}, u32[]{:S(2)}) copy-start(bf16[4096,512]{1,0:T(8,128)(2,1)} %get-tuple-element.219) | copy-start | bytes 12582916 | tf_op jit(solution)/shard_map/cond

commit v3 on v0

v3 whole, which is shorter than its diff:
```python
import functools
import math

import jax
import jax.numpy as jnp
from jax import lax
from jax.experimental import pallas as pl
from jax.experimental.pallas import tpu as pltpu
from jax.sharding import PartitionSpec as P

HEADS = 32
PROJECT = ["query", "keys", "values"]


epsilon = 1e-06


def gather_steps(count):
    bits = [1 << i for i in reversed(range(count.bit_length() - 1))]
    steps = []
    while bits:
        if len(bits) % 2:
            steps.append([bits[0]])
            bits = bits[1:]
        else:
            steps.append([bits[1], bits[0], bits[0] | bits[1]])
            bits = bits[2:]
    return steps


def gather_pieces(block, axis):
    count = lax.axis_size(axis)
    held = [(block[None], [0])]
    for masks in gather_steps(count):
        if len(held) > 2:
            piece = jnp.concatenate([one for one, _ in held], axis=0)
            held = [(piece, [s for _, sources in held for s in sources])]
        received = []
        for piece, sources in held:
            for mask in masks:
                route = [(i, i ^ mask) for i in range(count)]
                received.append((lax.ppermute(piece, axis, route), [s ^ mask for s in sources]))
        held = held + received
    return held


def gather_masks(count):
    held = [[0]]
    for masks in gather_steps(count):
        if len(held) > 2:
            held = [[s for sources in held for s in sources]]
        held = held + [[s ^ mask for s in sources] for sources in held for mask in masks]
    return [s for sources in held for s in sources]


def exchange(block, axis, first, second):
    rest = [i for i in range(lax.axis_size(axis)) if i not in (first, second)]
    route = [(first, second), (second, first)]
    for i in range(0, len(rest) - 1, 2):
        route += [(rest[i], rest[i + 1]), (rest[i + 1], rest[i])]
    return lax.ppermute(block, axis, route)


def in_order(me_ref, pieces, sources, full_ref):
    for ref, masks in zip(pieces, sources):
        width = ref.shape[2]
        for i, mask in enumerate(masks):
            start = pl.multiple_of((me_ref[0] ^ mask) * width, width)
            full_ref[:, pl.ds(start, width)] = ref[i]


def normalise_into(full_ref, gain_ref, normed_ref):
    width = full_ref.shape[1]
    tile = min(width, 512)
    total = jnp.zeros((full_ref.shape[0], 128), jnp.float32)
    for start in range(0, width, 128):
        part = full_ref[:, start : start + 128].astype(jnp.float32)
        total = total + part * part
    mean = jnp.sum(total, axis=1, keepdims=True) * (1.0 / width)
    inverse = lax.rsqrt(mean + epsilon)
    for start in range(0, width, tile):
        columns = slice(start, start + tile)
        gain = gain_ref[:, columns].astype(jnp.float32)
        normed_ref[:, columns] = (
            full_ref[:, columns].astype(jnp.float32) * inverse * gain
        ).astype(jnp.bfloat16)


def multiply_into(rows_ref, weight_ref, store):
    width = weight_ref.shape[1]
    tile = min(width, 256)

    @pl.loop(0, width // tile)
    def _(step):
        columns = pl.ds(pl.multiple_of(step * tile, tile), tile)
        store(
            columns,
            jnp.dot(rows_ref[...], weight_ref[:, columns], preferred_element_type=jnp.float32),
        )


def attend_into(lengths_ref, row_count, head_dim, query_ref, blocks, mix_ref):
    shape = (row_count, row_count)
    query_pos = lax.broadcasted_iota(jnp.int32, shape, 0)
    key_pos = lax.broadcasted_iota(jnp.int32, shape, 1)
    for micro in range(query_ref.shape[0] // row_count):
        rows = slice(micro * row_count, (micro + 1) * row_count)
        allowed = []
        for _, _, is_table in blocks:
            if is_table:
                allowed.append((key_pos <= query_pos) & (key_pos < lengths_ref[micro, 1]))
            else:
                allowed.append(key_pos < lengths_ref[micro, 0])
        for start in range(0, query_ref.shape[1], head_dim):
            columns = slice(start, start + head_dim)
            query = query_ref[rows, columns]
            exps = []
            for (keys_ref, _, _), mask in zip(blocks, allowed):
                scores = lax.dot_general(
                    query,
                    keys_ref[rows, columns],
                    (((1,), (1,)), ((), ())),
                    preferred_element_type=jnp.float32,
                )
                exps.append(jnp.where(mask, jnp.exp(scores), 0.0))
            total = sum(jnp.sum(one, axis=1, keepdims=True) for one in exps)
            mix = None
            for one, (_, values_ref, _) in zip(exps, blocks):
                weights = (one / total).astype(jnp.bfloat16)
                part = jnp.dot(
                    weights, values_ref[rows, columns], preferred_element_type=jnp.float32
                )
                mix = part if mix is None else mix + part
            mix_ref[rows, columns] = mix.astype(jnp.bfloat16)


def layer_kernel(plan, *refs):
    refs = list(refs)
    me_ref, lengths_ref = refs[:2]
    pieces = refs[2 : 2 + len(plan["sources"])]
    refs = refs[2 + len(plan["sources"]) :]
    gain_ref, refs = refs[0], refs[1:]
    weights, refs = refs[: len(plan["project"])], refs[len(plan["project"]) :]
    given, refs = refs[: len(plan["given"])], refs[len(plan["given"]) :]
    out_ref, full_ref, normed_ref = refs[:3]
    held = {}
    for ref, names in zip(given, plan["given"]):
        for i, name in enumerate(names):
            held[name] = ref.at[i]
    targets = refs[3:] if plan["attend"] else [out_ref.at[i] for i in range(len(weights))]
    if not plan["attend"] and plan["keep_own"]:
        out_ref[len(weights)] = pieces[0][0]
    in_order(me_ref, pieces, plan["sources"], full_ref)
    normalise_into(full_ref, gain_ref, normed_ref)
    for name, weight_ref, target in zip(plan["project"], weights, targets):
        scale = plan["scale"] if name == "query" else None

        def store(columns, value, target=target, scale=scale):
            if scale is not None:
                value = value * scale
            target[:, columns] = value.astype(jnp.bfloat16)

        multiply_into(normed_ref, weight_ref, store)
        held[name] = target
    if plan["attend"]:
        blocks = [(held["keys" + tag], held["values" + tag], is_table)
                  for tag, is_table in plan["attend"]]
        attend_into(
            lengths_ref, plan["rows"], plan["head_dim"], held["query"], blocks, out_ref
        )


def project_kernel(sources, me_ref, *refs):
    pieces, refs = refs[: len(sources)], refs[len(sources) :]
    weight_ref, stream_ref, out_ref, full_ref = refs
    in_order(me_ref, pieces, sources, full_ref)

    def store(columns, value):
        out_ref[:, columns] = (stream_ref[:, columns].astype(jnp.float32) + value).astype(
            jnp.bfloat16
        )

    multiply_into(full_ref, weight_ref, store)


VMEM = pl.BlockSpec(memory_space=pltpu.VMEM)
SMEM = pl.BlockSpec(memory_space=pltpu.SMEM)


def load_kernel(weight_ref, _, out_ref, sem):
    copy = pltpu.make_async_copy(weight_ref, out_ref, sem)
    copy.start()
    copy.wait()


def load(weight, earlier):
    size = 2 * weight.size
    return pl.pallas_call(
        load_kernel,
        out_shape=pltpu.VMEM(weight.shape, weight.dtype),
        in_specs=[pl.BlockSpec(memory_space=pl.ANY)] * 2,
        out_specs=VMEM,
        scratch_shapes=[pltpu.SemaphoreType.DMA(())],
        compiler_params=pltpu.CompilerParams(vmem_limit_bytes=1 << 20),
        cost_estimate=pl.CostEstimate(flops=0, bytes_accessed=2 * size, transcendentals=0),
    )(weight, earlier)


def near(array):
    return pltpu.with_memory_space_constraint(array, pltpu.VMEM)


def local(patches, table_ids, lengths, embed_table, norm_gain, w_query, w_key, w_value, w_out):
    section_count = lax.axis_size("section")
    section_index = lax.axis_index("section")
    half = section_count // 2
    micro_count, row_count, width_local = patches.shape
    width_full = w_query.shape[1]
    head_dim = width_full // HEADS
    score_scale = 1.0 / math.sqrt(head_dim)
    weight_of = {"query": w_query[0], "keys": w_key[0], "values": w_value[0]}
    out_weight = w_out[0]
    total_rows = micro_count * row_count
    vocab_local = embed_table.shape[0]
    me = lax.axis_index("tp").reshape(1)
    bf16 = jnp.bfloat16
    part = ((total_rows, width_local), bf16)

    def only(indices, body, operands, shape):
        return lax.cond(
            member(*indices), body, lambda *_: tuple(jnp.zeros(s, d) for s, d in shape), *operands
        )

    def member(*indices):
        taken = section_index == indices[0]
        for index in indices[1:]:
            taken = taken | (section_index == index)
        return taken

    def after(value, *earlier):
        return lax.optimization_barrier((value,) + earlier)[0]

    def look_up():
        local_ids = table_ids.reshape(-1) - section_index * vocab_local
        vocab_cols = lax.broadcasted_iota(jnp.int32, (total_rows, vocab_local), 1)
        one_hot = (local_ids[:, None] == vocab_cols).astype(bf16)
        return jnp.dot(one_hot, embed_table, preferred_element_type=jnp.float32).astype(bf16)

    def gather_and_load(block, project):
        held = gather_pieces(block, "tp")
        moments = [held[0][0], held[1][0], held[1][0]]
        return held, [load(weight_of[n], m) for n, m in zip(project, moments)]

    def layer(held, project, weights=None, given=(), attend=None, keep_own=False):
        plan = {
            "sources": [masks for _, masks in held],
            "project": project,
            "given": [names for _, names in given],
            "attend": attend,
            "keep_own": keep_own,
            "scale": score_scale,
            "rows": row_count,
            "head_dim": head_dim,
        }
        scratch = [pltpu.VMEM((total_rows, width_full), bf16)] * 2
        out_shape = part[0] if attend else (len(project) + keep_own,) + part[0]
        if attend:
            scratch += [pltpu.VMEM(*part)] * len(project)
        return pl.pallas_call(
            functools.partial(layer_kernel, plan),
            out_shape=jax.ShapeDtypeStruct(out_shape, bf16),
            in_specs=[SMEM, SMEM] + [VMEM] * (len(held) + 1 + len(project) + len(given)),
            out_specs=VMEM,
            scratch_shapes=scratch,
            compiler_params=pltpu.CompilerParams(vmem_limit_bytes=8 << 20),
            cost_estimate=pl.CostEstimate(
                flops=2 * total_rows * width_full * width_local * len(project),
                bytes_accessed=2 * width_full * width_local * len(project),
                transcendentals=0,
            ),
        )(
            me,
            lengths,
            *[piece for piece, _ in held],
            norm_gain,
            *(weights or [near(weight_of[name]) for name in project]),
            *[rows for rows, _ in given],
        )

    def finish(stream, mix):
        held = gather_pieces(mix, "tp")
        return pl.pallas_call(
            functools.partial(project_kernel, [masks for _, masks in held]),
            out_shape=jax.ShapeDtypeStruct(*part),
            in_specs=[SMEM] + [VMEM] * (len(held) + 2),
            out_specs=VMEM,
            scratch_shapes=[pltpu.VMEM((total_rows, width_full), bf16)],
            compiler_params=pltpu.CompilerParams(vmem_limit_bytes=8 << 20),
            cost_estimate=pl.CostEstimate(
                flops=2 * total_rows * width_full * width_local,
                bytes_accessed=2 * width_full * width_local,
                transcendentals=0,
            ),
        )(me, *[piece for piece, _ in held], near(out_weight), stream)

    def encode(stream):
        held, weights = gather_and_load(stream, PROJECT)
        mix = layer(held, PROJECT, weights, attend=[("", False)])
        return (finish(stream, mix),)

    def embed(found):
        own = lax.cond(section_index == 0, look_up, lambda: found)
        sent = lax.ppermute(own, "section", [(0, half), (half, 0)])
        return only(
            [half],
            lambda rows: (layer(gather_pieces(rows, "tp"), PROJECT, keep_own=True),),
            (own + sent,),
            (table_part,),
        )

    def look_up_and_add():
        found = look_up()
        others = list(range(1, section_count))
        total = found
        for shift in range(1, len(others)):
            route = [(s, others[(i + shift) % len(others)]) for i, s in enumerate(others)]
            total = total + lax.ppermute(found, "section", route)
        return total

    def stack(held):
        return jnp.concatenate([piece for piece, _ in held], axis=0)

    table_part = ((len(PROJECT) + 1,) + part[0], bf16)
    memory_part = ((lax.axis_size("tp"),) + part[0], bf16)
    memory_masks = gather_masks(lax.axis_size("tp"))
    pair_part = ((2,) + part[0], bf16)

    stream = patches.reshape(total_rows, width_local)
    (updated,) = only([0], encode, (stream,), (part,))
    result = updated
    found = lax.cond(section_index != 0, look_up_and_add, lambda: jnp.zeros(*part))
    table = None
    for index in range(half):
        if index:
            (updated,) = only([index], encode, (stream,), (part,))
            result = jnp.where(section_index == index, updated, result)
        stream = exchange(
            after(updated, found if table is None else table), "section", index, index + 1
        )
        if table is None:
            (table,) = only([0, half], embed, (after(found, stream),), (table_part,))

    (memory,) = only(
        [half], lambda rows: (stack(gather_pieces(rows, "tp")),), (stream,), (memory_part,)
    )
    for index in range(half, section_count):
        received = memory
        if index > half:
            (pair,) = only(
                [index],
                lambda rows: (layer([(rows, memory_masks)], ["keys", "values"]),),
                (received,),
                (pair_part,),
            )
            stream = exchange(after(updated, pair), "section", index - 1, index)
        if index + 1 < section_count:
            memory = exchange(memory, "section", index, index + 1)
        if index == half:

            def decode(rows, table):
                mix = layer(
                    [(rows, memory_masks)],
                    ["keys", "values"],
                    given=[(table, ["query", "keys_t", "values_t", "own"])],
                    attend=[("", False), ("_t", True)],
                )
                return (finish(table[len(PROJECT)], mix),)

            (updated,) = only([index], decode, (received, table), (part,))
        else:

            def decode(stream, pair):
                held, weights = gather_and_load(stream, PROJECT)
                mix = layer(
                    held,
                    PROJECT,
                    weights,
                    given=[(pair, ["keys_m", "values_m"])],
                    attend=[("_m", False), ("", True)],
                )
                return (finish(stream, mix),)

            (updated,) = only([index], decode, (stream, pair), (part,))
        result = jnp.where(section_index == index, updated, result)
    return result.reshape(1, micro_count, row_count, width_local)


def solution(mesh):
    return jax.shard_map(
        local,
        mesh=mesh,
        in_specs=(
            P(None, None, "tp"),
            P(),
            P(),
            P("section", "tp"),
            P("section", None),
            P("section", None, "tp"),
            P("section", None, "tp"),
            P("section", None, "tp"),
            P("section", None, "tp"),
        ),
        out_specs=P("section", None, None, "tp"),
        check_vma=False,
    )
```

time: 447 us -> 156 us (0.35)
  blocking collectives: 250 us -> 0 us
  starting transfers between devices: 6.46 us -> 117 us
  waiting for transfers between devices: 113 us -> 10.3 us
  matrix products: 46.6 us -> 4.99 us
  between operations: 13.4 us -> 0.06 us
  Pallas kernels: 0 us -> 12.4 us
  other arithmetic: 9.88 us -> 0.66 us
  local copies, waits for them, and re-layouts: 3.77 us -> 9.72 us
    all_gather x10 -> x0, blocking collectives: 250 us -> none  [the longest x5 128 us: advance(): full_rows = lax.all_gather(stream, 'tp', axis=1, tiled=True)]
    ppermute x5 -> x20, starting transfers between devices: 6.46 us -> 117 us  [the longest x4 98 us: exchange(): return lax.ppermute(block, axis, route)]
    ppermute x5 -> x20, waiting for transfers between devices: 81.7 us -> 10.3 us  [the longest x4 6.13 us: exchange(): return lax.ppermute(block, axis, route)]
    dot_general x31 -> x1, matrix products: 46.6 us -> 4.99 us  [look_up(): jnp.dot(one_hot, embed_table, preferred_element_type=jnp.float32)]
    psum x1 -> x0, waiting for transfers between devices: 31.1 us -> none  [local(): embedded = lax.psum(looked_up.astype(jnp.bfloat16), 'section')]
    pallas_call x0 -> x6, Pallas kernels: none -> 12.4 us  [the longest x2 8.46 us: layer(): pl.pallas_call(functools.partial(layer_kernel, plan), out_shape=jax.Shape...]
    cond x0 -> x10, local copies, waits for them, and re-layouts: none -> 7.37 us
    select_n x15 -> x1, other arithmetic: 6.3 us -> 0.65 us  [local(): result = jnp.where(section_index == index, updated, result)]
  transfers between devices with their start and end apart: 6 -> 20, of which waited for: 6 -> 8; matrix products, arithmetic and copies ran while one was open for 0% -> 0% of each run, Pallas kernels for 0% -> 2%
where the time goes in v3:
time: 156 us
  starting transfers between devices  117 us (75%)
  Pallas kernels  12.4 us (8%)
  waiting for transfers between devices  10.3 us (7%)
  local copies, waits for them, and re-layouts  9.72 us (6%)
  matrix products  4.99 us (3%)
    ppermute x4, starting transfers between devices, exchange(): return lax.ppermute(block, axis, route)  98 us
    ppermute x14, starting transfers between devices, gather_pieces(): lax.ppermute(piece, axis, route)  14.1 us
    pallas_call x2, Pallas kernels, layer(): pl.pallas_call(functools.partial(layer_kernel, plan), out_shape=jax.Shape...  8.46 us
    cond x10, local copies, waits for them, and re-layouts  7.37 us
    ppermute x4, waiting for transfers between devices, exchange(): return lax.ppermute(block, axis, route)  6.13 us
    ppermute x2, starting transfers between devices, look_up_and_add(): total = total + lax.ppermute(found, 'section', route)  5.28 us
    dot_general x1, matrix products, look_up(): jnp.dot(one_hot, embed_table, preferred_element_type=jnp.float32)  4.99 us
  transfers between devices with their start and end apart: 20, of which 8 were waited for; matrix products, arithmetic and copies ran while one was open for 0% of the time, Pallas kernels for 2%

profile of v3, /device:TPU:3, one launch (start us, length us, event | category | flops | bytes accessed | tf_op | source)
XLA Modules:
  0.0 155.7 jit_solution(4910637772094266833)
XLA Ops:
  0.0 0.7 copy-done.22
  0.7 11.7 %conditional.11 = (bf16[64,512]{1,0:T(8,128)(2,1)S(1)}) conditional(s32[]{:T(128)} %convert_element_type.38, () %tuple.75, (s32[]{:T(128)}, s32[2,32]{1,0:T(2,128)S(1)}, bf16[8192,512]{1,0:T(8,128)(2,1)}) %tuple.138), branch_computations={%region_2.0_spmd, %region_3.0_spmd} | conditional | flops 537493568 | bytes 9241960 | solution.py:341
  0.7 0.1 sub.22
  0.8 5.0 %fusion.1 = bf16[64,512]{1,0:T(8,128)(2,1)S(1)} fusion(bf16[8192,512]{1,0:T(8,128)(2,1)} %get-tuple-element.177, s32[64]{0:T(128)S(1)} %sub.22), kind=kOutput, calls=%fused_computation.2 | convolution fusion | flops 537427968 | bytes 8454400 | tf_op jit(solution)/shard_map/cond/branch_1_fun/dot_general | solution.py:247
  5.8 2.6 %collective-permute-start.64 = (bf16[64,512]{1,0:T(8,128)(2,1)S(1)}, bf16[64,512]{1,0:T(8,128)(2,1)S(1)}, u32[]{:S(2)}, u32[]{:S(2)}) collective-permute-start(bf16[64,512]{1,0:T(8,128)(2,1)S(1)} %fusion.1), channel_id=1, source_target_pairs={{8,24},{16,8},{24,16},{9,25},{17,9},{25,17},{10,26},{18,10},{26,18... | collective-permute-start | bytes 196616 | tf_op jit(solution)/shard_map/cond/branch_1_fun/ppermute | solution.py:327
  8.4 2.7 %collective-permute-start.63 = (bf16[64,512]{1,0:T(8,128)(2,1)S(1)}, bf16[64,512]{1,0:T(8,128)(2,1)S(1)}, u32[]{:S(2)}, u32[]{:S(2)}) collective-permute-start(bf16[64,512]{1,0:T(8,128)(2,1)S(1)} %fusion.1), channel_id=1, source_target_pairs={{8,16},{16,24},{24,8},{9,17},{17,25},{25,9},{10,18},{18,26},{26,10... | collective-permute-start | bytes 196616 | tf_op jit(solution)/shard_map/cond/branch_1_fun/ppermute | solution.py:327
  11.1 1.3 collective-permute-done.63
  12.4 1.6 %collective-permute-start.66 = (bf16[64,512]{1,0:T(8,128)(2,1)S(1)}, bf16[64,512]{1,0:T(8,128)(2,1)S(1)}, u32[]{:S(2)}, u32[]{:S(2)}) collective-permute-start(bf16[64,512]{1,0:T(8,128)(2,1)S(1)} %get-tuple-element.241), channel_id=1, source_target_pairs={{0,8},{8,0},{16,24},{24,16},{1,9},{9,1},{17,25},{25,17},{2,10},{10... | collective-permute-start | bytes 196616 | tf_op jit(solution)/shard_map/ppermute | solution.py:61
  14.0 0.9 collective-permute-done.66
  15.0 0.7 conditional.13
  15.0 0.7 broadcast.33
  15.7 34.1 %collective-permute-start.67 = (bf16[64,512]{1,0:T(8,128)(2,1)S(1)}, bf16[64,512]{1,0:T(8,128)(2,1)S(1)}, u32[]{:S(2)}, u32[]{:S(2)}) collective-permute-start(bf16[64,512]{1,0:T(8,128)(2,1)S(1)} %get-tuple-element.243), channel_id=1, source_target_pairs={{8,16},{16,8},{0,24},{24,0},{9,17},{17,9},{1,25},{25,1},{10,18},{1... | collective-permute-start | bytes 196616 | tf_op jit(solution)/shard_map/ppermute | solution.py:61
  49.8 2.2 %collective-permute-done.67 = bf16[64,512]{1,0:T(8,128)(2,1)S(1)} collective-permute-done((bf16[64,512]{1,0:T(8,128)(2,1)S(1)}, bf16[64,512]{1,0:T(8,128)(2,1)S(1)}, u32[]{:S(2)}, u32[]{:S(2)}) %collective-permute-start.67) | collective-permute-done | bytes 65568 | tf_op jit(solution)/shard_map/ppermute | solution.py:61
  52.1 0.8 conditional.14
  52.1 0.8 broadcast.35
  52.9 62.2 %collective-permute-start.68 = (bf16[8,64,512]{2,1,0:T(8,128)(2,1)}, bf16[8,64,512]{2,1,0:T(8,128)(2,1)S(1)}, u32[]{:S(2)}, u32[]{:S(2)}) collective-permute-start(bf16[8,64,512]{2,1,0:T(8,128)(2,1)} %get-tuple-element.245), channel_id=1, source_target_pairs={{16,24},{24,16},{0,8},{8,0},{17,25},{25,17},{1,9},{9,1},{18,26},{2... | collective-permute-start | bytes 1572872 | tf_op jit(solution)/shard_map/ppermute | solution.py:61
  115.1 1.7 %collective-permute-done.68 = bf16[8,64,512]{2,1,0:T(8,128)(2,1)S(1)} collective-permute-done((bf16[8,64,512]{2,1,0:T(8,128)(2,1)}, bf16[8,64,512]{2,1,0:T(8,128)(2,1)S(1)}, u32[]{:S(2)}, u32[]{:S(2)}) %collective-permute-start.68) | collective-permute-done | bytes 524320 | tf_op jit(solution)/shard_map/ppermute | solution.py:61
  116.9 7.2 %conditional.16 = (bf16[2,64,512]{2,1,0:T(8,128)(2,1)S(1)}) conditional(s32[]{:T(128)} %convert_element_type.34, () %tuple.84, (s32[1]{0:T(128)}, s32[2,2]{1,0:T(2,128)S(1)}, bf16[8,64,512]{2,1,0:T(8,128)(2,1)S(1)}, bf16[1,4096]{1,0:T(2,128)(2,1)S(1)}, bf16[4096,512]{1,0:T(8,128)(2,1)}, /*index=5*/bf16[4096,512]{1,0:T(8,128)(2,1)}) %tuple.136), branch_computations={%region_16.17_spmd, %region_17.18_spmd} | conditional | flops 536870912 | bytes 41943104 | solution.py:230
  116.9 2.2 %copy-done.4 = bf16[4096,512]{1,0:T(8,128)(2,1)S(1)} copy-done((bf16[4096,512]{1,0:T(8,128)(2,1)S(1)}, bf16[4096,512]{1,0:T(8,128)(2,1)}, u32[]{:S(2)}) %copy-start.4) | copy-done | bytes 4194328 | tf_op jit(solution)/shard_map/cond
  119.1 2.2 %copy-done.10 = bf16[4096,512]{1,0:T(8,128)(2,1)S(1)} copy-done((bf16[4096,512]{1,0:T(8,128)(2,1)S(1)}, bf16[4096,512]{1,0:T(8,128)(2,1)}, u32[]{:S(2)}) %copy-start.10) | copy-done | bytes 4194328 | tf_op jit(solution)/shard_map/cond
  121.3 2.8 %branch_1_fun.32 = bf16[2,64,512]{2,1,0:T(8,128)(2,1)S(1)} custom-call(s32[1]{0:T(128)} %get-tuple-element.215.refs_0_, s32[2,2]{1,0:T(2,128)S(1)} %get-tuple-element.216.refs_1_, bf16[8,64,512]{2,1,0:T(8,128)(2,1)S(1)} %get-tuple-element.217.refs_2_, bf16[1,4096]{1,0:T(2,128)(2,1)S(1)} %get-tuple-element.218.refs_3_, bf16[4096,512]{1,0:T(8,128)(2,1)S(1)} %copy-done.4, ...), custom_call_target="tpu_custom_call" | custom-call | flops 536870912 | bytes 8388608 | tf_op jit(solution)/shard_map/cond/branch_1_fun/pallas_call | solution.py:269
  124.1 0.1 collective-permute-start.69
  124.2 1.2 collective-permute-done.69
  125.4 29.7 %conditional.17 = (bf16[64,512]{1,0:T(8,128)(2,1)S(1)}) conditional(s32[]{:T(128)} %convert_element_type.34, () %tuple.69, (bf16[64,512]{1,0:T(8,128)(2,1)S(1)}, bf16[4096,512]{1,0:T(8,128)(2,1)}, bf16[4096,512]{1,0:T(8,128)(2,1)}, bf16[4096,512]{1,0:T(8,128)(2,1)}, s32[1]{0:T(128)}, /*index=5*/s32[2,2]{1,0:T(2,128)S(1)}, ...), branch_computations={%region_18.19_spmd, %region_19.20_spmd} | conditional | flops 1073741824 | bytes 95945360 | solution.py:230
  125.4 1.6 %collective-permute-start.28 = (bf16[1,64,512]{2,1,0:T(8,128)(2,1)S(1)}, bf16[1,64,512]{2,1,0:T(8,128)(2,1)S(1)}, u32[]{:S(2)}, u32[]{:S(2)}) collective-permute-start(bf16[1,64,512]{2,1,0:T(8,128)(2,1)S(1)} %bitcast.75), channel_id=1, source_target_pairs={{0,4},{1,5},{2,6},{3,7},{4,0},{5,1},{6,2},{7,3},{8,12},{9,13},{10,... | collective-permute-start | bytes 196616 | tf_op jit(solution)/shard_map/cond/branch_1_fun/ppermute | solution.py:42
  127.0 2.6 %collective-permute-start.31 = (bf16[1,64,512]{2,1,0:T(8,128)(2,1)S(1)}, bf16[1,64,512]{2,1,0:T(8,128)(2,1)S(1)}, u32[]{:S(2)}, u32[]{:S(2)}) collective-permute-start(bf16[1,64,512]{2,1,0:T(8,128)(2,1)S(1)} %bitcast.76), channel_id=1, source_target_pairs={{0,3},{1,2},{2,1},{3,0},{4,7},{5,6},{6,5},{7,4},{8,11},{9,10},{10,... | collective-permute-start | bytes 196616 | tf_op jit(solution)/shard_map/cond/branch_1_fun/ppermute | solution.py:42
  129.7 0.3 collective-permute-start.29
  130.0 2.4 %collective-permute-start.34 = (bf16[1,64,512]{2,1,0:T(8,128)(2,1)S(1)}, bf16[1,64,512]{2,1,0:T(8,128)(2,1)S(1)}, u32[]{:S(2)}, u32[]{:S(2)}) collective-permute-start(bf16[1,64,512]{2,1,0:T(8,128)(2,1)S(1)} %collective-permute-done.28._.refs_3_), channel_id=1, source_target_pairs={{0,3},{1,2},{2,1},{3,0},{4,7},{5,6},{6,5},{7,4},{8,11},{9,10},{10,... | collective-permute-start | bytes 196616 | tf_op jit(solution)/shard_map/cond/branch_1_fun/ppermute | solution.py:42
  132.3 0.3 collective-permute-start.32
  132.6 2.3 %branch_1_fun.33.refs_11_ = bf16[4096,512]{1,0:T(8,128)(2,1)S(1)} custom-call(bf16[4096,512]{1,0:T(8,128)(2,1)} %get-tuple-element.225.weight_ref, bf16[1,64,512]{2,1,0:T(8,128)(2,1)S(1)} %bitcast.79), custom_call_target="tpu_custom_call" | custom-call | bytes 8388608 | tf_op jit(solution)/shard_map/cond/branch_1_fun/pallas_call | solution.py:198
  135.0 1.1 copy-done.11
  136.1 0.3 branch_1_fun.35.refs_13_
  136.4 1.9 %copy-done.5 = bf16[4096,512]{1,0:T(8,128)(2,1)S(1)} copy-done((bf16[4096,512]{1,0:T(8,128)(2,1)S(1)}, bf16[4096,512]{1,0:T(8,128)(2,1)}, u32[]{:S(2)}) %copy-start.5) | copy-done | bytes 4194328 | tf_op jit(solution)/shard_map/cond
  138.3 0.3 branch_1_fun.34.refs_12_
  138.6 0.0 copy-start.15
  138.6 5.7 %branch_1_fun.36 = bf16[64,512]{1,0:T(8,128)(2,1)S(1)} custom-call(s32[1]{0:T(128)} %get-tuple-element.221.refs_0_.me_ref, s32[2,2]{1,0:T(2,128)S(1)} %get-tuple-element.222.refs_1_, bf16[1,64,512]{2,1,0:T(8,128)(2,1)S(1)} %bitcast.80, bf16[1,64,512]{2,1,0:T(8,128)(2,1)S(1)} %collective-permute-done.28._.refs_3_, ...), custom_call_target="tpu_custom_call" | custom-call | flops 805306368 | bytes 12582912 | tf_op jit(solution)/shard_map/cond/branch_1_fun/pallas_call | solution.py:269
  144.3 1.6 %collective-permute-start.35 = (bf16[1,64,512]{2,1,0:T(8,128)(2,1)S(1)}, bf16[1,64,512]{2,1,0:T(8,128)(2,1)S(1)}, u32[]{:S(2)}, u32[]{:S(2)}) collective-permute-start(bf16[1,64,512]{2,1,0:T(8,128)(2,1)S(1)} %bitcast.52), channel_id=1, source_target_pairs={{0,4},{1,5},{2,6},{3,7},{4,0},{5,1},{6,2},{7,3},{8,12},{9,13},{10,... | collective-permute-start | bytes 196616 | tf_op jit(solution)/shard_map/cond/branch_1_fun/ppermute | solution.py:42
  145.9 2.4 %collective-permute-start.38 = (bf16[1,64,512]{2,1,0:T(8,128)(2,1)S(1)}, bf16[1,64,512]{2,1,0:T(8,128)(2,1)S(1)}, u32[]{:S(2)}, u32[]{:S(2)}) collective-permute-start(bf16[1,64,512]{2,1,0:T(8,128)(2,1)S(1)} %bitcast.53), channel_id=1, source_target_pairs={{0,3},{1,2},{2,1},{3,0},{4,7},{5,6},{6,5},{7,4},{8,11},{9,10},{10,... | collective-permute-start | bytes 196616 | tf_op jit(solution)/shard_map/cond/branch_1_fun/ppermute | solution.py:42
  148.3 0.0 collective-permute-start.37
  148.3 0.3 collective-permute-start.36
  148.6 2.4 %collective-permute-start.41 = (bf16[1,64,512]{2,1,0:T(8,128)(2,1)S(1)}, bf16[1,64,512]{2,1,0:T(8,128)(2,1)S(1)}, u32[]{:S(2)}, u32[]{:S(2)}) collective-permute-start(bf16[1,64,512]{2,1,0:T(8,128)(2,1)S(1)} %collective-permute-done.35.refs_1_), channel_id=1, source_target_pairs={{0,3},{1,2},{2,1},{3,0},{4,7},{5,6},{6,5},{7,4},{8,11},{9,10},{10,... | collective-permute-start | bytes 196616 | tf_op jit(solution)/shard_map/cond/branch_1_fun/ppermute | solution.py:42
  150.9 0.3 collective-permute-start.39
  151.2 0.2 collective-permute-done.37.refs_3_
  151.4 1.2 collective-permute-done.41.refs_7_
  152.6 1.5 collective-permute-done.40.refs_6_
  154.0 0.0 collective-permute-done.39.refs_5_
  154.0 1.0 branch_1_fun.37
  155.1 0.6 select_select_fusion
  (32 shorter events, 0.1 us)
Async XLA Ops:
  0.0 0.7 copy-start.22
  0.7 14.3 %copy-start.18 = (bf16[1,4096]{1,0:T(2,128)(2,1)S(1)}, bf16[1,4096]{1,0:T(2,128)(2,1)}, u32[]{:S(2)}) copy-start(bf16[1,4096]{1,0:T(2,128)(2,1)} %param.33) | copy-start | bytes 24580
  0.7 14.3 %copy-start.20 = (s32[2,2]{1,0:T(2,128)S(1)}, s32[2,2]{1,0:T(2,128)}, u32[]{:S(2)}) copy-start(s32[2,2]{1,0:T(2,128)} %param.31) | copy-start | bytes 52
  5.8 5.3 %collective-permute-start.64 = (bf16[64,512]{1,0:T(8,128)(2,1)S(1)}, bf16[64,512]{1,0:T(8,128)(2,1)S(1)}, u32[]{:S(2)}, u32[]{:S(2)}) collective-permute-start(bf16[64,512]{1,0:T(8,128)(2,1)S(1)} %fusion.1), channel_id=1, source_target_pairs={{8,24},{16,8},{24,16},{9,25},{17,9},{25,17},{10,26},{18,10},{26,18... | collective-permute-start | bytes 196616 | tf_op jit(solution)/shard_map/cond/branch_1_fun/ppermute | solution.py:327
  8.4 4.0 %collective-permute-start.63 = (bf16[64,512]{1,0:T(8,128)(2,1)S(1)}, bf16[64,512]{1,0:T(8,128)(2,1)S(1)}, u32[]{:S(2)}, u32[]{:S(2)}) collective-permute-start(bf16[64,512]{1,0:T(8,128)(2,1)S(1)} %fusion.1), channel_id=1, source_target_pairs={{8,16},{16,24},{24,8},{9,17},{17,25},{25,9},{10,18},{18,26},{26,10... | collective-permute-start | bytes 196616 | tf_op jit(solution)/shard_map/cond/branch_1_fun/ppermute | solution.py:327
  12.4 2.5 %collective-permute-start.66 = (bf16[64,512]{1,0:T(8,128)(2,1)S(1)}, bf16[64,512]{1,0:T(8,128)(2,1)S(1)}, u32[]{:S(2)}, u32[]{:S(2)}) collective-permute-start(bf16[64,512]{1,0:T(8,128)(2,1)S(1)} %get-tuple-element.241), channel_id=1, source_target_pairs={{0,8},{8,0},{16,24},{24,16},{1,9},{9,1},{17,25},{25,17},{2,10},{10... | collective-permute-start | bytes 196616 | tf_op jit(solution)/shard_map/ppermute | solution.py:61
  15.7 36.4 %collective-permute-start.67 = (bf16[64,512]{1,0:T(8,128)(2,1)S(1)}, bf16[64,512]{1,0:T(8,128)(2,1)S(1)}, u32[]{:S(2)}, u32[]{:S(2)}) collective-permute-start(bf16[64,512]{1,0:T(8,128)(2,1)S(1)} %get-tuple-element.243), channel_id=1, source_target_pairs={{8,16},{16,8},{0,24},{24,0},{9,17},{17,9},{1,25},{25,1},{10,18},{1... | collective-permute-start | bytes 196616 | tf_op jit(solution)/shard_map/ppermute | solution.py:61
  52.9 64.0 %collective-permute-start.68 = (bf16[8,64,512]{2,1,0:T(8,128)(2,1)}, bf16[8,64,512]{2,1,0:T(8,128)(2,1)S(1)}, u32[]{:S(2)}, u32[]{:S(2)}) collective-permute-start(bf16[8,64,512]{2,1,0:T(8,128)(2,1)} %get-tuple-element.245), channel_id=1, source_target_pairs={{16,24},{24,16},{0,8},{8,0},{17,25},{25,17},{1,9},{9,1},{18,26},{2... | collective-permute-start | bytes 1572872 | tf_op jit(solution)/shard_map/ppermute | solution.py:61
  116.9 2.2 %copy-start.4 = (bf16[4096,512]{1,0:T(8,128)(2,1)S(1)}, bf16[4096,512]{1,0:T(8,128)(2,1)}, u32[]{:S(2)}) copy-start(bf16[4096,512]{1,0:T(8,128)(2,1)} %get-tuple-element.219.refs_4_) | copy-start | bytes 12582916 | tf_op jit(solution)/shard_map/cond
  119.1 2.2 %copy-start.10 = (bf16[4096,512]{1,0:T(8,128)(2,1)S(1)}, bf16[4096,512]{1,0:T(8,128)(2,1)}, u32[]{:S(2)}) copy-start(bf16[4096,512]{1,0:T(8,128)(2,1)} %get-tuple-element.220.refs_5_) | copy-start | bytes 12582916 | tf_op jit(solution)/shard_map/cond
  124.1 1.3 collective-permute-start.69
  125.4 4.6 %collective-permute-start.28 = (bf16[1,64,512]{2,1,0:T(8,128)(2,1)S(1)}, bf16[1,64,512]{2,1,0:T(8,128)(2,1)S(1)}, u32[]{:S(2)}, u32[]{:S(2)}) collective-permute-start(bf16[1,64,512]{2,1,0:T(8,128)(2,1)S(1)} %bitcast.75), channel_id=1, source_target_pairs={{0,4},{1,5},{2,6},{3,7},{4,0},{5,1},{6,2},{7,3},{8,12},{9,13},{10,... | collective-permute-start | bytes 196616 | tf_op jit(solution)/shard_map/cond/branch_1_fun/ppermute | solution.py:42
  127.0 5.3 %collective-permute-start.31 = (bf16[1,64,512]{2,1,0:T(8,128)(2,1)S(1)}, bf16[1,64,512]{2,1,0:T(8,128)(2,1)S(1)}, u32[]{:S(2)}, u32[]{:S(2)}) collective-permute-start(bf16[1,64,512]{2,1,0:T(8,128)(2,1)S(1)} %bitcast.76), channel_id=1, source_target_pairs={{0,3},{1,2},{2,1},{3,0},{4,7},{5,6},{6,5},{7,4},{8,11},{9,10},{10,... | collective-permute-start | bytes 196616 | tf_op jit(solution)/shard_map/cond/branch_1_fun/ppermute | solution.py:42
  129.7 8.9 %collective-permute-start.30 = (bf16[1,64,512]{2,1,0:T(8,128)(2,1)S(1)}, bf16[1,64,512]{2,1,0:T(8,128)(2,1)S(1)}, u32[]{:S(2)}, u32[]{:S(2)}) collective-permute-start(bf16[1,64,512]{2,1,0:T(8,128)(2,1)S(1)} %bitcast.77), channel_id=1, source_target_pairs={{0,2},{1,3},{2,0},{3,1},{4,6},{5,7},{6,4},{7,5},{8,10},{9,11},{10,... | collective-permute-start | bytes 196616 | tf_op jit(solution)/shard_map/cond/branch_1_fun/ppermute | solution.py:42
  129.7 8.9 %collective-permute-start.29 = (bf16[1,64,512]{2,1,0:T(8,128)(2,1)S(1)}, bf16[1,64,512]{2,1,0:T(8,128)(2,1)S(1)}, u32[]{:S(2)}, u32[]{:S(2)}) collective-permute-start(bf16[1,64,512]{2,1,0:T(8,128)(2,1)S(1)} %bitcast.78), channel_id=1, source_target_pairs={{0,1},{1,0},{2,3},{3,2},{4,5},{5,4},{6,7},{7,6},{8,9},{9,8},{10,11... | collective-permute-start | bytes 196616 | tf_op jit(solution)/shard_map/cond/branch_1_fun/ppermute | solution.py:42
  130.0 8.6 %collective-permute-start.34 = (bf16[1,64,512]{2,1,0:T(8,128)(2,1)S(1)}, bf16[1,64,512]{2,1,0:T(8,128)(2,1)S(1)}, u32[]{:S(2)}, u32[]{:S(2)}) collective-permute-start(bf16[1,64,512]{2,1,0:T(8,128)(2,1)S(1)} %collective-permute-done.28._.refs_3_), channel_id=1, source_target_pairs={{0,3},{1,2},{2,1},{3,0},{4,7},{5,6},{6,5},{7,4},{8,11},{9,10},{10,... | collective-permute-start | bytes 196616 | tf_op jit(solution)/shard_map/cond/branch_1_fun/ppermute | solution.py:42
  132.3 6.3 %collective-permute-start.33 = (bf16[1,64,512]{2,1,0:T(8,128)(2,1)S(1)}, bf16[1,64,512]{2,1,0:T(8,128)(2,1)S(1)}, u32[]{:S(2)}, u32[]{:S(2)}) collective-permute-start(bf16[1,64,512]{2,1,0:T(8,128)(2,1)S(1)} %collective-permute-done.28._.refs_3_), channel_id=1, source_target_pairs={{0,2},{1,3},{2,0},{3,1},{4,6},{5,7},{6,4},{7,5},{8,10},{9,11},{10,... | collective-permute-start | bytes 196616 | tf_op jit(solution)/shard_map/cond/branch_1_fun/ppermute | solution.py:42
  132.3 6.3 %collective-permute-start.32 = (bf16[1,64,512]{2,1,0:T(8,128)(2,1)S(1)}, bf16[1,64,512]{2,1,0:T(8,128)(2,1)S(1)}, u32[]{:S(2)}, u32[]{:S(2)}) collective-permute-start(bf16[1,64,512]{2,1,0:T(8,128)(2,1)S(1)} %collective-permute-done.28._.refs_3_), channel_id=1, source_target_pairs={{0,1},{1,0},{2,3},{3,2},{4,5},{5,4},{6,7},{7,6},{8,9},{9,8},{10,11... | collective-permute-start | bytes 196616 | tf_op jit(solution)/shard_map/cond/branch_1_fun/ppermute | solution.py:42
  132.6 3.4 %copy-start.11 = (bf16[4096,512]{1,0:T(8,128)(2,1)S(1)}, bf16[4096,512]{1,0:T(8,128)(2,1)}, u32[]{:S(2)}) copy-start(bf16[4096,512]{1,0:T(8,128)(2,1)} %get-tuple-element.227.weight_ref) | copy-start | bytes 12582916 | tf_op jit(solution)/shard_map/cond
  136.1 2.2 %copy-start.5 = (bf16[4096,512]{1,0:T(8,128)(2,1)S(1)}, bf16[4096,512]{1,0:T(8,128)(2,1)}, u32[]{:S(2)}) copy-start(bf16[4096,512]{1,0:T(8,128)(2,1)} %get-tuple-element.226.weight_ref) | copy-start | bytes 12582916 | tf_op jit(solution)/shard_map/cond
  138.6 15.4 %copy-start.15 = (bf16[4096,512]{1,0:T(8,128)(2,1)S(1)}, bf16[4096,512]{1,0:T(8,128)(2,1)}, u32[]{:S(2)}) copy-start(bf16[4096,512]{1,0:T(8,128)(2,1)} %get-tuple-element.229.refs_8_) | copy-start | bytes 12582916 | tf_op jit(solution)/shard_map/cond
  144.3 4.3 %collective-permute-start.35 = (bf16[1,64,512]{2,1,0:T(8,128)(2,1)S(1)}, bf16[1,64,512]{2,1,0:T(8,128)(2,1)S(1)}, u32[]{:S(2)}, u32[]{:S(2)}) collective-permute-start(bf16[1,64,512]{2,1,0:T(8,128)(2,1)S(1)} %bitcast.52), channel_id=1, source_target_pairs={{0,4},{1,5},{2,6},{3,7},{4,0},{5,1},{6,2},{7,3},{8,12},{9,13},{10,... | collective-permute-start | bytes 196616 | tf_op jit(solution)/shard_map/cond/branch_1_fun/ppermute | solution.py:42
  145.9 5.0 %collective-permute-start.38 = (bf16[1,64,512]{2,1,0:T(8,128)(2,1)S(1)}, bf16[1,64,512]{2,1,0:T(8,128)(2,1)S(1)}, u32[]{:S(2)}, u32[]{:S(2)}) collective-permute-start(bf16[1,64,512]{2,1,0:T(8,128)(2,1)S(1)} %bitcast.53), channel_id=1, source_target_pairs={{0,3},{1,2},{2,1},{3,0},{4,7},{5,6},{6,5},{7,4},{8,11},{9,10},{10,... | collective-permute-start | bytes 196616 | tf_op jit(solution)/shard_map/cond/branch_1_fun/ppermute | solution.py:42
  148.3 3.1 %collective-permute-start.37 = (bf16[1,64,512]{2,1,0:T(8,128)(2,1)S(1)}, bf16[1,64,512]{2,1,0:T(8,128)(2,1)S(1)}, u32[]{:S(2)}, u32[]{:S(2)}) collective-permute-start(bf16[1,64,512]{2,1,0:T(8,128)(2,1)S(1)} %bitcast.54), channel_id=1, source_target_pairs={{0,2},{1,3},{2,0},{3,1},{4,6},{5,7},{6,4},{7,5},{8,10},{9,11},{10,... | collective-permute-start | bytes 196616 | tf_op jit(solution)/shard_map/cond/branch_1_fun/ppermute | solution.py:42
  148.3 3.1 %collective-permute-start.36 = (bf16[1,64,512]{2,1,0:T(8,128)(2,1)S(1)}, bf16[1,64,512]{2,1,0:T(8,128)(2,1)S(1)}, u32[]{:S(2)}, u32[]{:S(2)}) collective-permute-start(bf16[1,64,512]{2,1,0:T(8,128)(2,1)S(1)} %bitcast.55), channel_id=1, source_target_pairs={{0,1},{1,0},{2,3},{3,2},{4,5},{5,4},{6,7},{7,6},{8,9},{9,8},{10,11... | collective-permute-start | bytes 196616 | tf_op jit(solution)/shard_map/cond/branch_1_fun/ppermute | solution.py:42
  148.6 4.0 %collective-permute-start.41 = (bf16[1,64,512]{2,1,0:T(8,128)(2,1)S(1)}, bf16[1,64,512]{2,1,0:T(8,128)(2,1)S(1)}, u32[]{:S(2)}, u32[]{:S(2)}) collective-permute-start(bf16[1,64,512]{2,1,0:T(8,128)(2,1)S(1)} %collective-permute-done.35.refs_1_), channel_id=1, source_target_pairs={{0,3},{1,2},{2,1},{3,0},{4,7},{5,6},{6,5},{7,4},{8,11},{9,10},{10,... | collective-permute-start | bytes 196616 | tf_op jit(solution)/shard_map/cond/branch_1_fun/ppermute | solution.py:42
  150.9 3.1 %collective-permute-start.40 = (bf16[1,64,512]{2,1,0:T(8,128)(2,1)S(1)}, bf16[1,64,512]{2,1,0:T(8,128)(2,1)S(1)}, u32[]{:S(2)}, u32[]{:S(2)}) collective-permute-start(bf16[1,64,512]{2,1,0:T(8,128)(2,1)S(1)} %collective-permute-done.35.refs_1_), channel_id=1, source_target_pairs={{0,2},{1,3},{2,0},{3,1},{4,6},{5,7},{6,4},{7,5},{8,10},{9,11},{10,... | collective-permute-start | bytes 196616 | tf_op jit(solution)/shard_map/cond/branch_1_fun/ppermute | solution.py:42
  150.9 3.1 %collective-permute-start.39 = (bf16[1,64,512]{2,1,0:T(8,128)(2,1)S(1)}, bf16[1,64,512]{2,1,0:T(8,128)(2,1)S(1)}, u32[]{:S(2)}, u32[]{:S(2)}) collective-permute-start(bf16[1,64,512]{2,1,0:T(8,128)(2,1)S(1)} %collective-permute-done.35.refs_1_), channel_id=1, source_target_pairs={{0,1},{1,0},{2,3},{3,2},{4,5},{5,4},{6,7},{7,6},{8,9},{9,8},{10,11... | collective-permute-start | bytes 196616 | tf_op jit(solution)/shard_map/cond/branch_1_fun/ppermute | solution.py:42
